TPU v7x, 32 devices: a whole 2x2x4 slice. The times are simulated.
32 devices in a mesh: dp: 8 (over z, core), mp: 4 (over y, x).
Axes of the slice: x: 2, y: 2, z: 4, core: 2. Of those that a mesh axis runs over, the one named last changes fastest.
Arguments:
- tokens: bfloat16 [65536, 1024], P('dp'), may hold values from -7 to 7
- segments: int32 [64, 1024], P('dp'), may hold values from 0 to 3, never falling along the last dimension, each value on 1 to 512 neighbouring positions
- routes: int32 [64, 128], P('dp'), may hold values from 0 to 1023, as said below
- cotangent: bfloat16 [65536, 1024], P('dp'), may hold values from -6 to 6
- gain_attn: bfloat16 [1024], replicated, may hold values from 0.5 to 1.5
- gain_mlp: bfloat16 [1024], replicated, may hold values from 0.5 to 1.5
- w_router: bfloat16 [1024], replicated, may hold values from -1 to 1
- w_qkv: bfloat16 [1024, 3072], P(None, 'mp'), may hold values from -0.1875 to 0.1875
- w_out: bfloat16 [1024, 1024], P('mp'), may hold values from -0.75 to 0.75
- w_up: bfloat16 [1024, 4096], P(None, 'mp'), may hold values from -0.1875 to 0.1875
- w_down: bfloat16 [4096, 1024], P('mp'), may hold values from -0.09375 to 0.09375
Outputs:
- output: bfloat16 [65536, 1024], P('dp')
- grad_tokens: bfloat16 [65536, 1024], P('dp')
- grad_gain_attn: float32 [1024], replicated
- grad_gain_mlp: float32 [1024], replicated
- grad_router: float32 [1024], replicated
- grad_qkv: float32 [1024, 3072], P(None, 'mp')
- grad_out: float32 [1024, 1024], P('mp')
- grad_up: float32 [1024, 4096], P(None, 'mp')
- grad_down: float32 [4096, 1024], P('mp')
- routed_share: float32 [], replicated
- mean_score: float32 [], replicated
Inputs may be any that keep to these rules, and one draw needn't show every extreme that they name: `routes`: each row holds 128 different positions of its sequence in ascending order, the first 0 and the last 1023. The segment numbers of one sequence never fall; each of the 4 segments has 1 to 512 positions, one exactly 512.
All inputs are finite; a program needn't handle non-finite values.
Results may differ from a plain program's by a relative error of at most 0.012.
Values may be sent and summed in bfloat16 or wider, within the bound.
No kernel may reach another device: no remote copies, remote signals or barrier semaphores. Data moves between devices by JAX's collectives and lax.ppermute only.
A program may use at most 256 MiB of HBM per device.

v0:
```python
import functools

import jax
import jax.numpy as jnp
from jax import lax
from jax.experimental import pallas as pl
from jax.experimental.pallas import tpu as pltpu
from jax.sharding import PartitionSpec as P

HD = 64
EPS = 1e-06
SCALE = HD ** (-0.5)
GELU_C = (2.0 / 3.141592653589793) ** 0.5
GELU_A = 0.044715
F32 = jnp.float32
BF16 = jnp.bfloat16


def dot(left, right, on=((1,), (0,))):
    return lax.dot_general(left, right, (on, ((), ())), preferred_element_type=F32)


NT = ((1,), (1,))
TN = ((0,), (0,))


def iota(shape, axis):
    return lax.broadcasted_iota(jnp.int32, shape, axis)


def sigmoid(value):
    return 1.0 / (1.0 + jnp.exp(-value))


LENGTHS = {
    "front": 5.2, "cot": 3.2, "middle": 5.5, "rows": 2.8, "outs": 3.9, "back": 1.0,
    "delta": 0.01, "mlp": 0.01, "last": 0.33, "put_own": 0.01, "put_out": 2.4, "put_grad": 2.4, "join": 1.5,
}
RATE = 1.5e9


def call(body, grid, in_specs, out_specs, out_shape, flops, nbytes, name, scratch=(), alias=None):
    if flops == 1:
        flops = LENGTHS[name] * grid[0] * RATE
        nbytes = 1
    return pl.pallas_call(
        body,
        grid_spec=pltpu.PrefetchScalarGridSpec(
            num_scalar_prefetch=1,
            grid=grid,
            in_specs=in_specs,
            out_specs=out_specs,
            scratch_shapes=list(scratch),
        ),
        out_shape=out_shape,
        cost_estimate=pl.CostEstimate(
            flops=int(flops), bytes_accessed=int(nbytes), transcendentals=0
        ),
        input_output_aliases=alias or {},
        name=name,
    )


def whole(shape):
    zeros = (0,) * len(shape)
    return pl.BlockSpec(shape, lambda *_: zeros)


def one_hot_rows(routes_row, length):
    routed = routes_row.shape[1]
    eye = iota((routed, routed), 0) == iota((routed, routed), 1)
    column = jnp.sum(jnp.where(eye, routes_row.astype(F32), 0.0), axis=1, keepdims=True)
    return iota((routed, length), 1) == column.astype(jnp.int32), eye


def head_mask(hot, eye, seg_line):
    seg_col = jnp.sum(jnp.where(hot, seg_line, 0.0), axis=1, keepdims=True)
    seg_row = jnp.sum(jnp.where(eye, seg_col, 0.0), axis=0, keepdims=True)
    routed = eye.shape[0]
    causal = iota((routed, routed), 0) >= iota((routed, routed), 1)
    return causal & (seg_col == seg_row)


def softmax_head(query, key, allowed):
    logits = jnp.where(allowed, dot(query, key, NT) * SCALE, -1e30)
    expon = jnp.exp(logits - jnp.max(logits, axis=1, keepdims=True))
    return expon / jnp.sum(expon, axis=1, keepdims=True)


def front_body(
    heads, slice_rows, where, tokens, routes, segments, gain, router, w_qkv,
    xr_out, a1_out, qkv_out, mask_out, mixed_out, score_out,
):
    step = pl.program_id(0)
    length = tokens.shape[0]
    hot, eye = one_hot_rows(routes[pl.ds(step, 1), :], length)
    seg_line = segments[pl.ds(step, 1), :].astype(F32)
    allowed = head_mask(hot, eye, seg_line)
    mask_out[...] = jnp.where(allowed, 1.0, 0.0).astype(BF16)
    rows = dot(jnp.where(hot, 1.0, 0.0).astype(BF16), tokens[...])
    xr_out[...] = rows.astype(BF16)
    vec = router[...].astype(F32)
    start = pl.multiple_of(where[0] * slice_rows, slice_rows)
    part = tokens[pl.ds(start, slice_rows), :].astype(F32)
    total = jnp.sum(sigmoid(jnp.sum(part * vec, axis=1, keepdims=True)), axis=0, keepdims=True)
    chosen = jnp.sum(sigmoid(jnp.sum(rows * vec, axis=1, keepdims=True)), axis=0, keepdims=True)

    @pl.when(step == 0)
    def _():
        score_out[...] = jnp.zeros_like(score_out)

    which = iota(score_out.shape, 0)
    score_out[...] += jnp.where(which == 0, total, jnp.where(which == 1, chosen, 0.0))
    inverse = lax.rsqrt(jnp.mean(rows * rows, axis=1, keepdims=True) + EPS)
    normed = (rows * inverse * gain[...].astype(F32)).astype(BF16)
    a1_out[...] = normed
    joint = dot(normed, w_qkv[...]).astype(BF16)
    qkv_out[...] = joint
    for head in range(heads):
        base = head * 3 * HD
        query = joint[:, base : base + HD]
        key = joint[:, base + HD : base + 2 * HD]
        value = joint[:, base + 2 * HD : base + 3 * HD]
        probs = softmax_head(query, key, allowed).astype(BF16)
        mixed_out[:, head * HD : (head + 1) * HD] = dot(probs, value).astype(BF16)


def cot_body(where, cotangent, routes, xr, router, w_down, dyr_out, gm_out, dh_out):
    step = pl.program_id(0)
    hot, _ = one_hot_rows(routes[pl.ds(step, 1), :], cotangent.shape[0])
    rows = dot(jnp.where(hot, 1.0, 0.0).astype(BF16), cotangent[...])
    dyr_out[...] = rows.astype(BF16)
    vec = router[...].astype(F32)
    rate = sigmoid(jnp.sum(xr[...].astype(F32) * vec, axis=1, keepdims=True))
    low = (rate * rows).astype(BF16)
    gm_out[...] = low
    dh_out[...] = dot(low, w_down[...], NT)


def middle_body(parts, table, *refs):
    mixed = refs[:parts]
    w_out, xr, dh, gain, w_up = refs[parts : parts + 5]
    attn_out, a2_out, hid_out, du_out, da2_out, gain_out = refs[parts + 5 :]
    attn = dot(mixed[0][...], w_out[0])
    for part in range(1, parts):
        attn = attn + dot(mixed[part][...], w_out[part])
    attn_out[...] = attn
    y = xr[...].astype(F32) + attn
    scaled = y * lax.rsqrt(jnp.mean(y * y, axis=1, keepdims=True) + EPS)
    a2 = (scaled * gain[...].astype(F32)).astype(BF16)
    a2_out[...] = a2
    u = dot(a2, w_up[...])
    square = u * u
    t = jnp.tanh(GELU_C * (u + GELU_A * (u * square)))
    hid_out[...] = (0.5 * u * (1.0 + t)).astype(BF16)
    slope = 0.5 * (1.0 + t) + (0.5 * GELU_C) * u * (1.0 - t * t) * (1.0 + 3.0 * GELU_A * square)
    du = (dh[...] * slope).astype(BF16)
    du_out[...] = du
    da2 = dot(du, w_up[...], NT)
    da2_out[0] = da2.astype(BF16)

    @pl.when(pl.program_id(0) == 0)
    def _():
        gain_out[...] = jnp.zeros_like(gain_out)

    gain_out[...] += jnp.sum((da2 * scaled).reshape(-1, 8, da2.shape[1]), axis=0)


def rows_body(parts, where, *refs):
    pieces = refs[:parts]
    attn, xr, dyr, gain, router, w_out = refs[parts : parts + 6]
    dyn_out, ga_out, do_out = refs[parts + 6 :]
    da2 = pieces[0][...].astype(F32)
    for piece in pieces[1:]:
        da2 = da2 + piece[...].astype(F32)
    rows = xr[...].astype(F32)
    y = rows + attn[...]
    inverse = lax.rsqrt(jnp.mean(y * y, axis=1, keepdims=True) + EPS)
    t = gain[...].astype(F32) * da2
    scaled = y * inverse
    dyn = inverse * (t - scaled * jnp.mean(t * scaled, axis=1, keepdims=True))
    dyn_out[...] = dyn
    rate = sigmoid(jnp.sum(rows * router[...].astype(F32), axis=1, keepdims=True))
    ga = (rate * dyr[...].astype(F32) + dyn).astype(BF16)
    ga_out[...] = ga
    for part in range(parts):
        do_out[part] = dot(ga, w_out[part], NT).astype(BF16)


def delta_body(parts, where, *refs):
    pieces = refs[:parts]
    attn, xr, dyr, dyn, router = refs[parts : parts + 5]
    upd_out, base_out, grad_router_out = refs[parts + 5 :]
    delta = attn[...]
    for piece in pieces:
        delta = delta + piece[...].astype(F32)
    rows = xr[...].astype(F32)
    grads = dyr[...].astype(F32)
    vec = router[...].astype(F32)
    rate = sigmoid(jnp.sum(rows * vec, axis=1, keepdims=True))
    upd_out[...] = (rows + rate * delta).astype(BF16)
    dlogit = jnp.sum(grads * delta, axis=1, keepdims=True) * rate * (1.0 - rate)
    base_out[...] = grads + dyn[...] + dlogit * vec

    @pl.when(pl.program_id(0) == 0)
    def _():
        grad_router_out[...] = jnp.zeros_like(grad_router_out)

    grad_router_out[...] += jnp.sum((dlogit * rows).reshape(-1, 8, rows.shape[1]), axis=0)


def back_body(heads, where, qkv, mask, dmixed, xr, gain, w_qkv, dqkv_out, da1_out, gain_out):
    joint = qkv[...]
    allowed = mask[...].astype(F32) > 0.5
    grads = dmixed[0]
    pieces = []
    for head in range(heads):
        base = head * 3 * HD
        query = joint[:, base : base + HD]
        key = joint[:, base + HD : base + 2 * HD]
        value = joint[:, base + 2 * HD : base + 3 * HD]
        dmix = grads[:, head * HD : (head + 1) * HD]
        probs = softmax_head(query, key, allowed)
        dprobs = dot(dmix, value, NT)
        spread = jnp.sum(probs * dprobs, axis=1, keepdims=True)
        dlog = (probs * (dprobs - spread)).astype(BF16)
        dquery = dot(dlog, key) * SCALE
        dkey = dot(dlog, query, TN) * SCALE
        dvalue = dot(probs.astype(BF16), dmix, TN)
        pieces += [dquery.astype(BF16), dkey.astype(BF16), dvalue.astype(BF16)]
    for at, piece in enumerate(pieces):
        dqkv_out[:, at * HD : (at + 1) * HD] = piece
    da1 = dot(dqkv_out[...], w_qkv[...], NT)
    da1_out[0] = da1.astype(BF16)
    rows = xr[...].astype(F32)
    scaled = rows * lax.rsqrt(jnp.mean(rows * rows, axis=1, keepdims=True) + EPS)

    @pl.when(pl.program_id(0) == 0)
    def _():
        gain_out[...] = jnp.zeros_like(gain_out)

    gain_out[...] += jnp.sum((da1 * scaled).reshape(-1, 8, da1.shape[1]), axis=0)


def last_body(parts, where, *refs):
    pieces = refs[:parts]
    xr, base, gain = refs[parts : parts + 3]
    (out,) = refs[parts + 3 :]
    da1 = pieces[0][...].astype(F32)
    for piece in pieces[1:]:
        da1 = da1 + piece[...].astype(F32)
    rows = xr[...].astype(F32)
    inverse = lax.rsqrt(jnp.mean(rows * rows, axis=1, keepdims=True) + EPS)
    t = gain[...].astype(F32) * da1
    scaled = rows * inverse
    dxn = inverse * (t - scaled * jnp.mean(t * scaled, axis=1, keepdims=True))
    out[...] = (base[...] + dxn).astype(BF16)


def put_body(where, source, routes, rows, *refs):
    out = refs[-1]
    length = source.shape[0]
    at = where[pl.program_id(0)]
    line = routes[pl.ds(at, 1), :]
    hot = iota((length, line.shape[1]), 0) == line
    picked = jnp.where(hot, 1.0, 0.0)
    taken = jnp.sum(picked, axis=1, keepdims=True) > 0.5
    moved = dot(picked.astype(BF16), rows[...])
    out[...] = jnp.where(taken, moved, source[...].astype(F32)).astype(BF16)


def put_rows(source, routes, rows, order, target, name):
    seqs, routed = routes.shape
    length = source.shape[0] // seqs
    width = source.shape[1]
    count = rows.shape[0] // routed
    in_specs = [
        pl.BlockSpec((length, width), lambda i, w: (w[i], 0)),
        whole(routes.shape),
        pl.BlockSpec((routed, width), lambda i, w: (i, 0)),
    ]
    args = [order, source, routes, rows]
    alias = None
    if target is not None:
        in_specs.append(pl.BlockSpec(memory_space=pl.ANY))
        args.append(target)
        alias = {4: 0}
    return call(
        put_body,
        (count,),
        in_specs,
        pl.BlockSpec((length, width), lambda i, w: (w[i], 0)),
        jax.ShapeDtypeStruct(source.shape, BF16),
        2 * count * length * routed * width,
        count * length * width * 4,
        name,
        alias=alias,
    )(*args)


def swap(value, axis, offset):
    size = lax.axis_size(axis)
    return lax.ppermute(value, axis, [(i, i ^ offset) for i in range(size)])


def block_of(value, index, rows):
    return lax.dynamic_slice_in_dim(value, index * rows, rows, 0)


def in_core_order(core, mine, other):
    return jnp.where(
        core == 0,
        jnp.concatenate([mine, other], axis=0),
        jnp.concatenate([other, mine], axis=0),
    )


def line_sum(value, depth):
    at = lax.axis_index("dp") // 2
    half = depth // 2

    def shift(array, pairs):
        return lax.ppermute(
            array, "dp", [(2 * a + c, 2 * b + c) for a, b in pairs for c in range(2)]
        )

    def mirrored(a, b):
        return [(a, b), (depth - 1 - a, depth - 1 - b)]

    for step in range(half - 1):
        got = shift(value, mirrored(step, step + 1))
        value = (value.astype(F32) + got.astype(F32)).astype(BF16)
    if depth > 1:
        got = shift(value, mirrored(half - 1, half))
        value = (value.astype(F32) + got.astype(F32)).astype(BF16)
    for step in reversed(range(half - 1)):
        got = shift(value, mirrored(step + 1, step))
        here = (at == step) | (at == depth - 1 - step)
        value = jnp.where(here, got, value)
    return value


def core_half(value, core):
    half = value.shape[0] // 2
    keep = block_of(value, core, half)
    give = block_of(value, 1 - core, half)
    got = swap(give.astype(BF16), "dp", 1)
    return (keep.astype(F32) + got.astype(F32)).astype(BF16)


def core_join(value, core):
    return in_core_order(core, value, swap(value, "dp", 1)).astype(F32)


def general(
    tokens, segments, routes, cotangent, gain_attn, gain_mlp, w_router, w_qkv, w_out, w_up, w_down
):
    seqs, length = segments.shape
    routed = routes.shape[1]
    width = tokens.shape[1]
    total = seqs * routed
    wide = w_out.shape[0]
    heads = wide // HD
    joint = w_qkv.shape[1]
    hidden = w_up.shape[1]
    parts = lax.axis_size("mp")
    depth = lax.axis_size("dp") // 2
    own = total // parts
    rank = lax.axis_index("mp")
    core = lax.axis_index("dp") % 2
    aligned = own % routed == 0
    per = own // routed if aligned else 1
    where = rank.reshape(1).astype(jnp.int32)
    gain_one = gain_attn.reshape(1, width)
    gain_two = gain_mlp.reshape(1, width)
    router = w_router.reshape(1, width)
    partners = list(range(1, parts))
    sds = jax.ShapeDtypeStruct

    share = block_of(w_out, core, wide // 2)
    mine = jnp.stack([swap(share, "mp", j) for j in partners])
    other = swap(mine, "dp", 1)
    w_all = jnp.where(
        core == 0,
        jnp.concatenate([mine, other], axis=1),
        jnp.concatenate([other, mine], axis=1),
    )
    w_all = jnp.concatenate([w_out[None], w_all], axis=0)

    xr, a1, qkv, mask, mixed, score = call(
        functools.partial(front_body, heads, length // parts),
        (seqs,),
        [
            pl.BlockSpec((length, width), lambda i, w: (i, 0)),
            whole(routes.shape),
            whole(segments.shape),
            whole((1, width)),
            whole((1, width)),
            whole(w_qkv.shape),
        ],
        [
            pl.BlockSpec((routed, width), lambda i, w: (i, 0)),
            pl.BlockSpec((routed, width), lambda i, w: (i, 0)),
            pl.BlockSpec((routed, joint), lambda i, w: (i, 0)),
            pl.BlockSpec((routed, routed), lambda i, w: (i, 0)),
            pl.BlockSpec((routed, wide), lambda i, w: (i, 0)),
            whole((8, 128)),
        ],
        [
            sds((total, width), BF16),
            sds((total, width), BF16),
            sds((total, joint), BF16),
            sds((total, routed), BF16),
            sds((total, wide), BF16),
            sds((8, 128), F32),
        ],
        2 * total * width * (length + joint) * 1.3,
        2 * seqs * length * width + 8 * total * width,
        "front",
    )(where, tokens, routes, segments, gain_one, router, w_qkv)

    mixed_all = [mixed] + [swap(mixed, "mp", j) for j in partners]

    dyr, gm, dh = call(
        cot_body,
        (seqs,),
        [
            pl.BlockSpec((length, width), lambda i, w: (i, 0)),
            whole(routes.shape),
            pl.BlockSpec((routed, width), lambda i, w: (i, 0)),
            whole((1, width)),
            whole(w_down.shape),
        ],
        [
            pl.BlockSpec((routed, width), lambda i, w: (i, 0)),
            pl.BlockSpec((routed, width), lambda i, w: (i, 0)),
            pl.BlockSpec((routed, hidden), lambda i, w: (i, 0)),
        ],
        [sds((total, width), BF16), sds((total, width), BF16), sds((total, hidden), F32)],
        2 * total * width * (length + hidden),
        2 * seqs * length * width + 6 * total * width + 4 * total * hidden,
        "cot",
    )(where, cotangent, routes, xr, router, w_down)

    order = partners[::-1] + [0]
    tile = min(own, 128)
    tiles = own // tile
    blocks = jnp.stack([rank ^ j for j in order])
    table = (blocks[:, None] * tiles + jnp.arange(tiles)[None, :]).reshape(-1).astype(jnp.int32)

    def by_row(i, t):
        return (t[i], 0)

    steps = parts * tiles
    attn, a2, hid, du, da2, gain_two_part = call(
        functools.partial(middle_body, parts),
        (steps,),
        [pl.BlockSpec((tile, wide), by_row)] * parts
        + [
            whole(w_all.shape),
            pl.BlockSpec((tile, width), by_row),
            pl.BlockSpec((tile, hidden), by_row),
            whole((1, width)),
            whole(w_up.shape),
        ],
        [
            pl.BlockSpec((tile, width), lambda i, t: (jnp.maximum(i - (steps - tiles), 0), 0)),
            pl.BlockSpec((tile, width), by_row),
            pl.BlockSpec((tile, hidden), by_row),
            pl.BlockSpec((tile, hidden), by_row),
            pl.BlockSpec((1, tile, width), lambda i, t: (i // tiles, i % tiles, 0)),
            whole((8, width)),
        ],
        [
            sds((own, width), F32),
            sds((total, width), BF16),
            sds((total, hidden), BF16),
            sds((total, hidden), BF16),
            sds((parts, own, width), BF16),
            sds((8, width), F32),
        ],
        2 * total * width * (parts * wide + 2 * hidden),
        total * (10 * width + 8 * hidden) + 2 * width * (hidden + parts * wide),
        "middle",
    )(table, *mixed_all, w_all, xr, dh, gain_two, w_up)

    da2_all = [da2[-1]] + [swap(da2[at], "mp", j) for at, j in enumerate(order[:-1])]

    mlp = dot(hid, w_down).astype(BF16)
    grad_up = dot(a2, du, TN).astype(BF16)
    grad_down = dot(hid, gm, TN).astype(BF16)
    mlp_all = [block_of(mlp, rank, own)] + [
        swap(block_of(mlp, rank ^ j, own), "mp", j) for j in partners
    ]

    own_tiles = lambda i, w: (w[0] * tiles + i, 0)
    flat = lambda i, w: (i, 0)
    row_block = pl.BlockSpec((tile, width), flat)
    own_block = pl.BlockSpec((tile, width), own_tiles)
    dyn, ga, dmix = call(
        functools.partial(rows_body, parts),
        (tiles,),
        [row_block] * parts
        + [row_block, own_block, own_block, whole((1, width)), whole((1, width)), whole(w_all.shape)],
        [row_block, row_block, pl.BlockSpec((parts, tile, wide), lambda i, w: (0, i, 0))],
        [sds((own, width), F32), sds((own, width), BF16), sds((parts, own, wide), BF16)],
        2 * own * width * parts * wide,
        own * width * 24 + 2 * width * width,
        "rows",
    )(where, *da2_all, attn, xr, dyr, gain_two, router, w_all)

    dmix_all = jnp.stack([dmix[0]] + [swap(dmix[j], "mp", j) for j in partners])

    upd, base, router_part = call(
        functools.partial(delta_body, parts),
        (tiles,),
        [row_block] * parts + [row_block, own_block, own_block, row_block, whole((1, width))],
        [row_block, row_block, whole((8, width))],
        [sds((own, width), BF16), sds((own, width), F32), sds((8, width), F32)],
        own * width * 20,
        own * width * 24,
        "delta",
    )(where, *mlp_all, attn, xr, dyr, dyn, router)
    upd_all = [upd] + [swap(upd, "mp", j) for j in partners]

    if aligned:
        by_owner = lambda i, w: ((i // per) ^ w[0], i % per, 0)
        da1_shape = (parts, own, width)
    else:
        dmix_all = dmix_all[jnp.arange(parts) ^ rank].reshape(1, total, wide)
        by_owner = lambda i, w: (0, i, 0)
        da1_shape = (1, total, width)
    dqkv, da1, gain_one_part = call(
        functools.partial(back_body, heads),
        (seqs,),
        [
            pl.BlockSpec((routed, joint), flat),
            pl.BlockSpec((routed, routed), flat),
            pl.BlockSpec((1, routed, wide), by_owner),
            pl.BlockSpec((routed, width), flat),
            whole((1, width)),
            whole(w_qkv.shape),
        ],
        [
            pl.BlockSpec((routed, joint), flat),
            pl.BlockSpec((1, routed, width), by_owner),
            whole((8, width)),
        ],
        [sds((total, joint), BF16), sds(da1_shape, BF16), sds((8, width), F32)],
        2 * total * width * joint * 1.5,
        total * (4 * joint + 6 * width) + 2 * width * joint,
        "back",
    )(where, qkv, mask, dmix_all, xr, gain_one, w_qkv)

    if aligned:
        da1_blocks = [da1[j] for j in range(parts)]
    else:
        da1_blocks = [block_of(da1[0], rank ^ j, own) for j in range(parts)]
    da1_all = [da1_blocks[0]] + [swap(da1_blocks[j], "mp", j) for j in partners]

    grad_qkv = dot(a1, dqkv, TN).astype(BF16)

    last = call(
        functools.partial(last_body, parts),
        (tiles,),
        [row_block] * parts + [own_block, row_block, whole((1, width))],
        row_block,
        sds((own, width), BF16),
        own * width * 20,
        own * width * 18,
        "last",
    )(where, *da1_all, xr, base, gain_one)
    last_all = [last] + [swap(last, "mp", j) for j in partners]

    def spread(source, rows_all, name):
        if not aligned:
            rows = jnp.stack(rows_all)[jnp.arange(parts) ^ rank].reshape(total, width)
            return put_rows(source, routes, rows, jnp.arange(seqs, dtype=jnp.int32), None, name)
        target = None
        for j, rows in enumerate(rows_all):
            seq = ((rank ^ j) * per + jnp.arange(per)).astype(jnp.int32)
            target = put_rows(source, routes, rows, seq, target, name)
        return target

    output = spread(tokens, upd_all, "put_out")
    grad_tokens = spread(cotangent, last_all, "put_grad")

    grad_up = core_join(line_sum(core_half(grad_up, core), depth), core)
    grad_down = core_join(line_sum(core_half(grad_down, core), depth), core)
    grad_qkv = core_join(line_sum(core_half(grad_qkv, core), depth), core)

    def out_part(j):
        rows = block_of(mixed_all[j], rank, own)
        return dot(rows, ga, TN).astype(BF16)

    outs = jnp.stack([out_part(j) for j in range(parts)], axis=1)
    outs = core_half(outs, core)
    half = outs[:, 0].astype(F32)
    for j in partners:
        half = half + swap(outs[:, j], "mp", j).astype(F32)
    grad_out = core_join(line_sum(half.astype(BF16), depth), core)

    lines = jnp.sum(
        jnp.stack([gain_one_part, gain_two_part, router_part]), axis=1
    )
    scores = jnp.concatenate(
        [score[0:1] / 1.0, score[1:2] / parts, jnp.zeros((6, 128), F32)], axis=0
    ).reshape(1, -1)
    scores = jnp.pad(scores, ((0, 0), (0, width - 1024))) if width > 1024 else scores[:, :width]
    small = jnp.concatenate([lines, scores, jnp.zeros((4, width), F32)], axis=0)
    bit = 1
    while bit < 2 * depth:
        small = small + swap(small, "dp", bit)
        bit *= 2
    bit = 1
    while bit < parts:
        small = small + swap(small, "mp", bit)
        bit *= 2
    score_total = small[3, 0]
    routed_total = small[3, 128]
    token_count = seqs * length * lax.axis_size("dp")
    return (
        output,
        grad_tokens,
        small[0],
        small[1],
        small[2],
        grad_qkv,
        grad_out,
        grad_up,
        grad_down,
        routed_total / score_total,
        score_total / token_count,
    )


STREAMS = ((1, 3, 0, 2), (2, 3, 0, 1))
FIRST = (1, 2)


def row(vector):
    return vector[...].astype(F32).reshape(1, -1)

def owner_spec(stream, rows, columns, slots=()):
    lead = tuple(slots)
    zeros = (0,) * len(lead)
    if stream == 0:
        return pl.BlockSpec(
            lead + (2, None, None, rows, columns), lambda i, w: zeros + (0, 1 - i, 0, 0, 0)
        )
    return pl.BlockSpec(
        lead + (None, 2, None, rows, columns), lambda i, w: zeros + (1 - i, 0, 1, 0, 0)
    )


def joined(value):
    return value.reshape(-1, value.shape[-1])


def parted(value):
    return value.reshape(2, -1, value.shape[-1])


def front_pair_body(heads, slice_rows, first, where, *refs):
    blocks = refs[:2]
    routes, segments, gain, router, w_qkv = refs[2:7]
    xr_out, give_out, keep_out, qkv_out, mask_out, lse_out, mixed_out, score_out = refs[-8:]
    step = pl.program_id(0)
    length, width = blocks[0].shape
    routed = routes.shape[1]
    vec = jnp.broadcast_to(row(router), (8, width)).astype(BF16)
    start = pl.multiple_of(where[RANK] * slice_rows, slice_rows)
    rows_all, allowed_all = [], []
    total = jnp.zeros((8, 1), F32)
    for at, tokens in enumerate(blocks):
        seq = where[first + 2 * step + at]
        hot, eye = one_hot_rows(routes[pl.ds(seq, 1), :], length)
        seg_line = segments[pl.ds(seq, 1), :].astype(F32)
        allowed = head_mask(hot, eye, seg_line)
        mask_out[at * routed : (at + 1) * routed, :] = jnp.where(allowed, 1.0, 0.0).astype(BF16)
        rows_all.append(dot(jnp.where(hot, 1.0, 0.0).astype(BF16), tokens[...]))
        allowed_all.append(allowed)
        scored = sigmoid(dot(vec, tokens[pl.ds(start, slice_rows), :], NT))
        total = total + jnp.sum(scored, axis=1, keepdims=True)
    rows = jnp.concatenate(rows_all, axis=0)
    low = rows.astype(BF16)
    xr_out[...] = parted(low)
    chosen = jnp.sum(sigmoid(dot(vec, low, NT)), axis=1, keepdims=True)

    @pl.when(step == 0)
    def _():
        score_out[...] = jnp.zeros_like(score_out)

    which = iota(score_out.shape, 0)
    score_out[...] += jnp.where(which == 0, total, jnp.where(which == 1, chosen, 0.0))
    inverse = lax.rsqrt(jnp.mean(rows * rows, axis=1, keepdims=True) + EPS)
    normed = (rows * inverse * row(gain)).astype(BF16)
    left, right = parted(normed[:, : width // 2]), parted(normed[:, width // 2 :])
    give_out[...] = jnp.where(where[CORE] == 0, right, left)
    keep_out[...] = jnp.where(where[CORE] == 0, left, right)
    joint = dot(normed, w_qkv[...]).astype(BF16)
    qkv_out[...] = joint
    logits = []
    for at in range(2):
        own = joint[at * routed : (at + 1) * routed]
        for head in range(heads):
            base = head * 3 * HD
            raw = dot(own[:, base : base + HD], own[:, base + HD : base + 2 * HD], NT)
            logits.append(jnp.where(allowed_all[at], raw * SCALE, -1e30))
    logits = jnp.concatenate(logits, axis=0)
    top = jnp.max(logits, axis=1, keepdims=True)
    expon = jnp.exp(logits - top)
    norm = jnp.sum(expon, axis=1, keepdims=True)
    sums = top + jnp.log(norm)
    probs = (expon * (1.0 / norm)).astype(BF16)
    for at in range(2):
        span = slice(at * routed, (at + 1) * routed)
        for head in range(heads):
            place = slice((at * heads + head) * routed, (at * heads + head + 1) * routed)
            base = head * 3 * HD
            value = joint[span, base + 2 * HD : base + 3 * HD]
            lse_out[span, head : head + 1] = sums[place]
            mixed_out[span, head * HD : (head + 1) * HD] = dot(probs[place], value).astype(BF16)


def cot_pair_body(where, *refs):
    blocks = refs[:2]
    routes, xr, router, w_down, dyr_out, gm_out, dh_out = refs[2:]
    step = pl.program_id(0)
    length = blocks[0].shape[0]
    picked = []
    for at, block in enumerate(blocks):
        hot, _ = one_hot_rows(routes[pl.ds(where[PUT + 2 * step + at], 1), :], length)
        picked.append(dot(jnp.where(hot, 1.0, 0.0).astype(BF16), block[...]))
    rows = jnp.concatenate(picked, axis=0)
    dyr_out[...] = rows.astype(BF16)
    rate = sigmoid(jnp.sum(xr[...].astype(F32) * row(router), axis=1, keepdims=True))
    low = (rate * rows).astype(BF16)
    gm_out[...] = low
    dh_out[...] = dot(low, w_down[...], NT)


def flip(value, swapped):
    half = value.shape[0] // 2
    if swapped:
        return jnp.concatenate([value[half:], value[:half]], axis=0)
    return value


def middle_pair_body(stream, where, *refs):
    mixed = refs[:4]
    w_parts = refs[4:8]
    xr, dh, gm, gain, w_up = refs[8:13]
    attn_out, left_give, left_keep, right_give, right_keep, hid_out, send_out, keep_out = refs[-8:]
    step = pl.program_id(0)
    plain = (0, FIRST[stream])
    attn = 0.0
    for part in range(4):
        attn = attn + dot(flip(mixed[part][...], part not in plain), w_parts[part][...])
    half = attn.shape[0] // 2
    attn_out[...] = attn[:half]
    y = joined(xr[...]).astype(F32) + attn
    scaled = y * lax.rsqrt(jnp.mean(y * y, axis=1, keepdims=True) + EPS)
    a2 = (scaled * row(gain)).astype(BF16)
    u = dot(a2, w_up[...])
    square = u * u
    t = jnp.tanh(u * (GELU_C + (GELU_C * GELU_A) * square))
    cdf = 0.5 + 0.5 * t
    hid = (u * cdf).astype(BF16)
    hid_out[...] = parted(hid)
    slope = cdf + (u * (1.0 - t * t)) * (0.5 * GELU_C + (1.5 * GELU_C * GELU_A) * square)
    du = (joined(dh[...]) * slope).astype(BF16)
    low = dot(du, w_up[...], NT).astype(BF16)
    first = where[CORE] == 0
    left_give[...] = parted(jnp.where(first, a2, hid))
    left_keep[...] = parted(jnp.where(first, hid, a2))
    down = joined(gm[...])
    right_give[...] = parted(jnp.where(first, du, down))
    right_keep[...] = parted(jnp.where(first, down, du))

    @pl.when(step == 0)
    def _():
        send_out[0] = low[:half]
        send_out[1] = low[half:]

    @pl.when(step == 1)
    def _():
        keep_out[0] = low[:half]
        keep_out[1] = low[half:]


def mlp_body(where, hid, w_down, *outs):
    value = dot(hid[...], w_down[...]).astype(BF16)
    for at, out in enumerate(outs):

        @pl.when(pl.program_id(0) == at)
        def _(out=out):
            out[...] = value


def either(step, left, right):
    return jnp.where(step == 0, left, right).astype(F32)


def summed(step, refs):
    keep, first, final = [
        either(step, refs[at][...], refs[3 + at][...]) for at in range(3)
    ]
    return joined(keep) + joined(first) + final


def fold(value):
    return jnp.sum(value.reshape(-1, 8, value.shape[1]), axis=0)


def collect(step, out, value):
    @pl.when(step == 0)
    def _():
        out[...] = jnp.zeros_like(out)

    out[...] += value


def rows_pair_body(where, *refs):
    step = pl.program_id(0)
    da2 = summed(step, refs[:6])
    attn_a, attn_b, xr, dyr, gain, router = refs[6:12]
    w_parts = refs[12:16]
    dyn_out, ga_out, gain_out, do_outs = refs[16], refs[17], refs[18], refs[19:]
    rows = xr[...].astype(F32)
    y = rows + either(step, attn_a[...], attn_b[...])
    inverse = lax.rsqrt(jnp.mean(y * y, axis=1, keepdims=True) + EPS)
    scaled = y * inverse
    joint = da2 * scaled
    collect(step, gain_out, fold(joint))
    vec = row(gain)
    dyn = inverse * (vec * da2 - scaled * jnp.mean(vec * joint, axis=1, keepdims=True))
    dyn_out[...] = dyn
    rate = sigmoid(jnp.sum(rows * row(router), axis=1, keepdims=True))
    ga = (rate * dyr[...].astype(F32) + dyn).astype(BF16)
    ga_out[...] = ga
    for weight, out in zip(w_parts, do_outs):
        out[...] = dot(ga, weight[...], NT).astype(BF16)


def delta_pair_body(where, *refs):
    attn_a, attn_b, xr, dyr, dyn, router = refs[4:10]
    upd_out, base_out, grad_router_out = refs[10:]
    step = pl.program_id(0)
    delta = either(step, attn_a[...], attn_b[...])
    for piece in refs[:4]:
        delta = delta + piece[...].astype(F32)
    rows = xr[...].astype(F32)
    grads = dyr[...].astype(F32)
    vec = row(router)
    rate = sigmoid(jnp.sum(rows * vec, axis=1, keepdims=True))
    upd_out[...] = (rows + rate * delta).astype(BF16)
    dlogit = jnp.sum(grads * delta, axis=1, keepdims=True) * rate * (1.0 - rate)
    base_out[...] = grads + dyn[...] + dlogit * vec
    collect(step, grad_router_out, fold(dlogit * rows))


def out_grad_body(where, *refs):
    ga, keep_out, give_out = refs[8:]
    half = keep_out.shape[1]
    grads = ga[...]
    for out, core in ((keep_out, where[CORE]), (give_out, 1 - where[CORE])):
        span = pl.ds(pl.multiple_of(core * half, half), half)
        for at, part in enumerate(STREAMS[0]):
            mixed = jnp.concatenate([refs[part][:, span], refs[4 + part][:, span]], axis=0)
            out[at] = dot(mixed, grads, TN).astype(BF16)


def back_pair_body(heads, stream, where, qkv, mask, lse, *refs):
    dmixed = refs[:4]
    w_qkv = refs[4]
    dqkv_out, send_out, keep_out = refs[-3:]
    step = pl.program_id(0)
    owners = STREAMS[stream]
    routed = mask.shape[1]
    logits, dprobs, norms, items = [], [], [], []
    for at in range(2):
        span = slice(at * routed, (at + 1) * routed)
        joint = qkv[span, :]
        allowed = mask[span, :].astype(F32) > 0.5
        grads = jnp.where(step == 0, dmixed[owners[at]][...], dmixed[owners[2 + at]][...])
        for head in range(heads):
            base = head * 3 * HD
            query = joint[:, base : base + HD]
            key = joint[:, base + HD : base + 2 * HD]
            value = joint[:, base + 2 * HD : base + 3 * HD]
            dmix = grads[:, head * HD : (head + 1) * HD]
            logits.append(jnp.where(allowed, dot(query, key, NT) * SCALE, -1e30))
            dprobs.append(dot(dmix, value, NT))
            norms.append(lse[span, head : head + 1])
            items.append((span, base, query, key, dmix))
    probs = jnp.exp(jnp.concatenate(logits, axis=0) - jnp.concatenate(norms, axis=0))
    dprobs = jnp.concatenate(dprobs, axis=0)
    spread = jnp.sum(probs * dprobs, axis=1, keepdims=True)
    dlogs = (probs * (dprobs - spread)).astype(BF16)
    probs = probs.astype(BF16)
    for at, (span, base, query, key, dmix) in enumerate(items):
        part = span.start // routed
        dlog = dlogs[at * routed : (at + 1) * routed]
        prob = probs[at * routed : (at + 1) * routed]
        dqkv_out[part, :, base : base + HD] = (dot(dlog, key) * SCALE).astype(BF16)
        dqkv_out[part, :, base + HD : base + 2 * HD] = (dot(dlog, query, TN) * SCALE).astype(BF16)
        dqkv_out[part, :, base + 2 * HD : base + 3 * HD] = dot(prob, dmix, TN).astype(BF16)
    low = dot(joined(dqkv_out[...]), w_qkv[...], NT).astype(BF16)

    @pl.when(step == 0)
    def _():
        send_out[0] = low[:routed]
        send_out[1] = low[routed:]

    @pl.when(step == 1)
    def _():
        keep_out[0] = low[:routed]
        keep_out[1] = low[routed:]


def last_pair_body(where, *refs):
    xr, base, gain, gain_two, router_part, score_a, score_b, out, gain_sum = refs[6:]
    step = pl.program_id(0)

    @pl.when(step < 2)
    def _():
        da1 = summed(step, refs[:6])
        rows = xr[...].astype(F32)
        inverse = lax.rsqrt(jnp.mean(rows * rows, axis=1, keepdims=True) + EPS)
        scaled = rows * inverse
        joint = da1 * scaled
        collect(step, gain_sum, fold(joint))
        vec = row(gain)
        dxn = inverse * (vec * da1 - scaled * jnp.mean(vec * joint, axis=1, keepdims=True))
        out[...] = (base[...] + dxn).astype(BF16)

    @pl.when(step == 2)
    def _():
        width = out.shape[1]
        scores = score_a[...] + score_b[...]
        scores = jnp.concatenate(
            [scores[0:1], scores[1:2] / 4, jnp.zeros((1, width - 256), F32)], axis=1
        )
        at = iota((16, width), 0)
        small = jnp.zeros((16, width), F32)
        lines = [gain_sum[...], gain_two[...], router_part[...]]
        lines = [jnp.sum(line, axis=0, keepdims=True) for line in lines] + [scores]
        for index, line in enumerate(lines):
            small = jnp.where(at % 8 == index, line, small)
        high = small.astype(BF16).astype(F32)
        out[:16, :] = jnp.where(at < 8, high, small - high).astype(BF16)


def place_body(starts, where, source, routes, *refs):
    rows, out = refs[: len(starts)], refs[-1]
    step = pl.program_id(0)
    line = routes[pl.ds(where[PUT + put_entry(starts, step)], 1), :]
    fresh = rows[0][...]
    for at, start in enumerate(starts):
        if at:
            fresh = jnp.where(step >= start[0], rows[at][...], fresh)
    chunk = min(256, source.shape[0])

    def place(at, carry):
        first = pl.multiple_of(at * chunk, chunk)
        hot = iota((chunk, line.shape[1]), 0) + first == line
        picked = jnp.where(hot, 1.0, 0.0)
        taken = jnp.sum(picked, axis=1, keepdims=True) > 0.5
        moved = dot(picked.astype(BF16), fresh)
        span = pl.ds(first, chunk)
        out[span, :] = jnp.where(taken, moved, source[span, :].astype(F32)).astype(BF16)
        return carry

    lax.fori_loop(0, source.shape[0] // chunk, place, 0)


def put_entry(starts, step):
    entry = starts[0][1] + step
    for first, place in starts[1:]:
        entry = jnp.where(step >= first, place + step - first, entry)
    return entry


def place_rows(table, source, routes, parts, target, name):
    seqs, routed = routes.shape
    length = source.shape[0] // seqs
    width = source.shape[1]
    starts, step = [], 0
    block = lambda i, w: (w[PUT + put_entry(starts, i)], 0)
    in_specs = [pl.BlockSpec((length, width), block), whole(routes.shape)]
    args = [table, source, routes]
    for rows, place in parts:
        per = rows.shape[0] // routed
        starts.append((step, place))
        in_specs.append(
            pl.BlockSpec(
                (routed, width),
                lambda i, w, first=step, top=per - 1: (jnp.clip(i - first, 0, top), 0),
            )
        )
        args.append(rows)
        step += per
    alias = None
    if target is not None:
        in_specs.append(pl.BlockSpec(memory_space=pl.ANY))
        alias = {len(args): 0}
        args.append(target)
    return call(
        functools.partial(place_body, tuple(starts)),
        (step,),
        in_specs,
        pl.BlockSpec((length, width), block),
        jax.ShapeDtypeStruct(source.shape, BF16),
        1,
        1,
        name,
        alias=alias,
    )(*args)


def halves_body(where, value, side, pair, corner, down_out, up_out):
    step = pl.program_id(0)
    for late, (own, other) in enumerate(((value, pair), (side, corner))):
        for core, outs in enumerate(((down_out, up_out), (up_out, down_out))):

            @pl.when((step // 2 == late) & (where[CORE] == core))
            def _(own=own, other=other, outs=outs):
                outs[0][...] = own[...].astype(F32)
                outs[1][...] = other[...].astype(F32)


def join_halves(table, pieces):
    rows, columns = pieces[0].shape
    block = (rows // 2, columns)
    early = pl.BlockSpec(block, lambda i, w: (jnp.minimum(i, 1), 0))
    late = pl.BlockSpec(block, lambda i, w: (jnp.maximum(i - 2, 0), 0))
    placed = pl.BlockSpec(block, lambda i, w: (2 * (w[BIT] ^ (i // 2)) + i % 2, 0))
    value, pair, side, corner = pieces
    return call(
        halves_body,
        (4,),
        [early, late, early, late],
        [placed, placed],
        [jax.ShapeDtypeStruct((2 * rows, columns), F32)] * 2,
        1,
        1,
        "join",
    )(table, value, side, pair, corner)


def tail_body(where, *refs):
    qkv_out, out_out = refs[-2:]
    for at in range(4):

        @pl.when(pl.program_id(0) == at)
        def _(at=at):
            qkv_out[...] = refs[at][...].astype(F32)
            if at < 2:
                out_out[...] = refs[4 + at][...].astype(F32)


def join_tail(table, pieces, outs):
    rows, columns = pieces[0].shape
    few, wide = outs[0].shape
    return call(
        tail_body,
        (4,),
        [whole((rows, columns))] * 4 + [whole((few, wide))] * 2,
        [
            pl.BlockSpec((rows, columns), lambda i, w: (w[QUARTER + i], 0)),
            pl.BlockSpec((few, wide), lambda i, w: (w[14 + jnp.minimum(i, 1)], 0)),
        ],
        [
            jax.ShapeDtypeStruct((4 * rows, columns), F32),
            jax.ShapeDtypeStruct((2 * few, wide), F32),
        ],
        1,
        1,
        "join",
    )(table, *pieces, *outs)


def after(value, *others):
    return lax.optimization_barrier((value, *others))[0]


def add(left, right):
    return (left.astype(F32) + right.astype(F32)).astype(BF16)


class Total:
    def __init__(self, give, keep, bit):
        self.keep, self.bit = keep, bit
        self.sent = swap(give, "dp", 1)

    def split(self, *others):
        got = after(self.sent, *others)
        rows = got.shape[0] // 2
        cut = lambda index: add(block_of(self.keep, index, rows), block_of(got, index, rows))
        far = cut(1 - self.bit)
        self.value = cut(self.bit)
        self.sent = swap(far, "dp", 2)
        return far

    def cross(self, *others):
        self.value = add(self.value, after(self.sent, *others))
        self.sent = swap(self.value, "dp", 4)
        return self.value

    def close(self, *others):
        self.value = add(self.value, after(self.sent, *others))
        self.sent = swap(self.value, "dp", 2)
        return self.value

    def share(self, *others):
        self.pair = swap(after(self.value, *others), "dp", 1)

    def back(self, *others):
        self.side = after(self.sent, *others)
        self.corner = swap(self.side, "dp", 1)
        return self.side

    def pieces(self):
        return [self.value, self.pair, self.side, self.corner]


OWNERS = (1, 3, 0, 2, 2, 3, 0, 1)
HALVES = (0, 0, 0, 0, 1, 1, 1, 1)
RANK, CORE, QUARTER, PUT, BIT = 8, 9, 10, 16, 24


def make_table(rank, core, bit):
    owners = jnp.array(OWNERS + (0,) * 8 + (0, 0, 1, 1, 2, 2, 3, 3, 0), jnp.int32)
    halves = jnp.array(HALVES + (0,) * 8 + (0, 1) * 4 + (0,), jnp.int32)
    at = jnp.arange(25, dtype=jnp.int32)
    table = 2 * (rank ^ owners) + halves
    quarter = at - QUARTER
    quarters = 2 * (core ^ (quarter % 2)) + (bit ^ (quarter // 2))
    table = jnp.where((at >= QUARTER) & (at < QUARTER + 4), quarters, table)
    table = jnp.where(at == 14, core, jnp.where(at == 15, 1 - core, table))
    table = jnp.where(at == BIT, bit, table)
    return jnp.where(at == RANK, rank, jnp.where(at == CORE, core, table)).astype(jnp.int32)


def paired(
    tokens, segments, routes, cotangent, gain_attn, gain_mlp, w_router, w_qkv, w_out, w_up, w_down
):
    seqs, length = segments.shape
    routed = routes.shape[1]
    width = tokens.shape[1]
    wide = w_out.shape[0]
    heads = wide // HD
    joint = w_qkv.shape[1]
    hidden = w_up.shape[1]
    rank = lax.axis_index("mp")
    core = lax.axis_index("dp") % 2
    bit = lax.axis_index("dp") // 2 % 2
    half_rows = 4 * routed
    pair = 2 * routed
    total_rows = 8 * routed
    sds = jax.ShapeDtypeStruct
    flat = lambda i, w: (i, 0)
    line = whole((width,))
    table = make_table(rank, core, bit)
    anywhere = pl.BlockSpec(memory_space=pl.ANY)
    partners = (1, 2, 3)

    def held(columns, dtype=BF16):
        return sds((2, 2, 2, routed, columns), dtype)

    def rowed(value):
        return value.reshape(total_rows, value.shape[-1])

    def by_owner(value):
        return value.reshape(2, 2, 2, routed, value.shape[-1])

    w_parts = [w_out] + [swap(w_out, "mp", j) for j in partners]

    fronts = []
    for stream in range(2):
        carried = fronts[0][:3] if fronts else []
        fronts.append(
            call(
                functools.partial(front_pair_body, heads, length // 4, 4 * stream),
                (2,),
                [
                    pl.BlockSpec((length, width), lambda i, w, s=4 * stream: (w[2 * i + s], 0)),
                    pl.BlockSpec((length, width), lambda i, w, s=4 * stream: (w[2 * i + 1 + s], 0)),
                    whole(routes.shape),
                    whole(segments.shape),
                    line,
                    line,
                    whole(w_qkv.shape),
                ]
                + [anywhere] * len(carried),
                [
                    owner_spec(stream, routed, width),
                    owner_spec(stream, routed, width // 2),
                    owner_spec(stream, routed, width // 2),
                    pl.BlockSpec((pair, joint), flat),
                    pl.BlockSpec((pair, routed), flat),
                    pl.BlockSpec((pair, 128), flat),
                    pl.BlockSpec((pair, wide), flat),
                    whole((8, 128)),
                ],
                [
                    held(width),
                    held(width // 2),
                    held(width // 2),
                    sds((half_rows, joint), BF16),
                    sds((half_rows, routed), BF16),
                    sds((half_rows, 128), F32),
                    sds((half_rows, wide), BF16),
                    sds((8, 128), F32),
                ],
                1,
                1,
                "front",
                alias={8 + at: at for at in range(len(carried))},
            )(
                after(table, fronts[0][6]) if fronts else table,
                tokens, tokens, routes, segments, gain_attn, w_router, w_qkv, *carried,
            )
        )
    xr, a1_give, a1_keep = fronts[1][:3]
    qkv, mask, lse, heads_out, score = [list(kind) for kind in zip(*[f[3:] for f in fronts])]
    xr_rows = rowed(xr)

    dyr, gm, dh = call(
        cot_pair_body,
        (4,),
        [
            pl.BlockSpec((length, width), lambda i, w: (w[PUT + 2 * i], 0)),
            pl.BlockSpec((length, width), lambda i, w: (w[PUT + 2 * i + 1], 0)),
            whole(routes.shape),
            pl.BlockSpec((pair, width), flat),
            line,
            whole(w_down.shape),
        ],
        [
            pl.BlockSpec((pair, width), flat),
            pl.BlockSpec((pair, width), flat),
            pl.BlockSpec((pair, hidden), flat),
        ],
        [
            sds((total_rows, width), BF16),
            sds((total_rows, width), BF16),
            sds((total_rows, hidden), F32),
        ],
        1,
        1,
        "cot",
    )(table, cotangent, cotangent, routes, xr_rows, w_router, w_down)

    w_parts = [w_out] + [after(weight, heads_out[1]) for weight in w_parts[1:]]
    mixed = []
    for stream in range(2):
        near, far = FIRST[stream], FIRST[1 - stream]
        rows = after(heads_out[1], *w_parts[1:]) if stream else heads_out[0]
        beside = swap(rows, "mp", near)
        across = swap(rows, "mp", far)
        came = after(beside, gm) if stream else after(beside, *w_parts[1:])
        corner = swap(came, "mp", far)
        parts = [heads_out[stream], None, None, corner]
        parts[near], parts[far] = came, across
        mixed.append(parts)

    middles = []
    for stream in range(2):
        near = FIRST[stream]
        specs = []
        for part in range(4):
            crossed = part in (near, 3)
            specs.append(
                pl.BlockSpec((pair, wide), (lambda i, w: (1 - i, 0)) if crossed else flat)
            )
        carried = middles[0][1:6] if middles else []
        middles.append(
            call(
                functools.partial(middle_pair_body, stream),
                (2,),
                specs
                + [whole(w_out.shape)] * 4
                + [
                    owner_spec(stream, routed, width),
                    owner_spec(stream, routed, hidden),
                    owner_spec(stream, routed, width),
                    line,
                    whole(w_up.shape),
                ]
                + [anywhere] * len(carried),
                [whole((routed, width))]
                + [owner_spec(stream, routed, width)] * 5
                + [whole((2, routed, width))] * 2,
                [sds((routed, width), F32)]
                + [held(width)] * 5
                + [sds((2, routed, width), BF16)] * 2,
                1,
                1,
                "middle",
                alias={14 + at: 1 + at for at in range(len(carried))},
            )(
                after(table, middles[0][7]) if middles else table,
                *mixed[stream], *w_parts, xr, by_owner(dh), by_owner(gm), gain_mlp, w_up, *carried,
            )
        )
    attn = [middles[0][0], middles[1][0]]
    left_give, left_keep, right_give, right_keep, hid = [rowed(v) for v in middles[1][1:6]]
    send, keep = [[m[at] for m in middles] for at in (6, 7)]

    first_a = after(swap(send[0], "mp", FIRST[0]), keep[1])
    ahead_a = add(keep[0][1], first_a[1])
    final_a = swap(ahead_a, "mp", FIRST[1])

    ffn_give = dot(after(left_give, ahead_a), right_give, TN).astype(BF16)
    mlp = call(
        mlp_body,
        (4,),
        [pl.BlockSpec((pair, hidden), flat), whole(w_down.shape)],
        [whole((pair, width))] * 4,
        [sds((pair, width), BF16)] * 4,
        1,
        1,
        "mlp",
    )(after(table, ffn_give), hid, w_down)
    first_b = after(swap(send[1], "mp", FIRST[1]), mlp[0])
    ahead_b = add(keep[1][1], first_b[1])
    final_b = swap(ahead_b, "mp", FIRST[0])
    ffn_keep = dot(after(left_keep, ahead_b), right_keep, TN).astype(BF16)
    ffn = Total(after(ffn_give, ahead_b), ffn_keep, bit)
    ffn_far = ffn.split(ffn_keep)
    mlp_all = [mlp[0], swap(after(mlp[1], ahead_b), "mp", 1), None, None]

    part = pl.BlockSpec((routed, width), flat)
    pieces = [
        pl.BlockSpec((1, routed, width), lambda i, w: (0, 0, 0)),
        pl.BlockSpec((1, routed, width), lambda i, w: (0, 0, 0)),
        whole((routed, width)),
    ] * 2
    rows_out = call(
        rows_pair_body,
        (2,),
        pieces + [whole((routed, width))] * 2 + [part, part, line, line] + [whole(w_out.shape)] * 4,
        [part, part, whole((8, width))] + [pl.BlockSpec((routed, wide), flat)] * 4,
        [sds((pair, width), F32), sds((pair, width), BF16), sds((8, width), F32)]
        + [sds((pair, wide), BF16)] * 4,
        1,
        1,
        "rows",
    )(
        after(table, ffn_far), keep[0], first_a, final_a, keep[1], first_b,
        final_b, *attn, xr_rows, dyr, gain_mlp, w_router, *w_parts,
    )
    dyn, ga, gain_two_part = rows_out[:3]
    dmix = [rows_out[3]] + [swap(rows_out[3 + j], "mp", j) for j in partners]

    out_specs = [
        pl.BlockSpec((routed, wide), lambda i, w, at=STREAMS[s].index(j): (at, 0))
        for s in (0, 1)
        for j in range(4)
    ]
    outs_keep, outs_give = call(
        out_grad_body,
        (1,),
        out_specs + [whole((pair, width))],
        [whole((4, wide // 2, width))] * 2,
        [sds((4, wide // 2, width), BF16)] * 2,
        1,
        1,
        "outs",
    )(after(table, ga), *mixed[0], *mixed[1], ga)
    outs_got = swap(outs_give, "dp", 1)
    dmix = [dmix[0]] + [after(value, outs_keep) for value in dmix[1:]]
    mlp_all[1] = after(mlp_all[1], *dmix[1:])
    mlp_all[2] = swap(after(mlp[2], mlp_all[1]), "mp", 2)
    mlp_all[3] = swap(after(mlp[3], mlp_all[1]), "mp", 3)
    ffn_now = ffn.cross(mlp_all[1])

    backs = []
    for stream in range(2):
        cut = pl.BlockSpec((routed, wide), lambda i, w, s=stream: (s, 0))
        carried = backs[0][:1] if backs else []
        backs.append(
            call(
                functools.partial(back_pair_body, heads, stream),
                (2,),
                [
                    pl.BlockSpec((pair, joint), flat),
                    pl.BlockSpec((pair, routed), flat),
                    pl.BlockSpec((pair, 128), flat),
                    cut,
                    cut,
                    cut,
                    cut,
                    whole(w_qkv.shape),
                ]
                + [anywhere] * len(carried),
                [
                    owner_spec(stream, routed, joint),
                    whole((2, routed, width)),
                    whole((2, routed, width)),
                ],
                [
                    held(joint),
                    sds((2, routed, width), BF16),
                    sds((2, routed, width), BF16),
                ],
                1,
                1,
                "back",
                alias={9: 0} if carried else None,
            )(
                after(table, backs[0][2]) if backs else after(table, ffn_now),
                qkv[stream], mask[stream], lse[stream], *dmix, w_qkv, *carried,
            )
        )
    dqkv = rowed(backs[1][0])
    back_send, back_keep = [[b[at] for b in backs] for at in (1, 2)]
    mlp_all[2] = after(mlp_all[2], back_keep[1])
    outs_got = after(outs_got, back_keep[1])
    qkv_give = dot(rowed(a1_give), dqkv, TN).astype(BF16)
    last_first_a = after(swap(back_send[0], "mp", FIRST[0]), qkv_give)
    last_ahead_a = add(back_keep[0][1], last_first_a[1])
    last_final_a = swap(last_ahead_a, "mp", FIRST[1])
    qkv_keep = dot(rowed(after(a1_keep, last_ahead_a)), dqkv, TN).astype(BF16)
    whole_qkv = Total(qkv_give, qkv_keep, bit)
    outs_x = add(after(outs_keep, qkv_keep)[:2], outs_got[:2])
    outs_sent = swap(outs_x, "mp", 1)
    mlp_all[3] = after(mlp_all[3], outs_x)

    upd, base, router_part = call(
        delta_pair_body,
        (2,),
        [part] * 4 + [whole((routed, width))] * 2 + [part] * 3 + [line],
        [part, part, whole((8, width))],
        [sds((pair, width), BF16), sds((pair, width), F32), sds((8, width), F32)],
        1,
        1,
        "delta",
    )(after(table, outs_x), *mlp_all, *attn, xr_rows, dyr, dyn, w_router)

    last_first_b = after(swap(back_send[1], "mp", FIRST[1]), base)
    last_ahead_b = add(back_keep[1][1], last_first_b[1])
    last_final_b = swap(last_ahead_b, "mp", FIRST[0])

    outs_sent = after(outs_sent, last_ahead_b)

    def outs_of(at, *more):
        value = outs_keep[2 + at].astype(F32) + outs_got[2 + at].astype(F32)
        for other in (outs_sent[at], *more):
            value = value + other.astype(F32)
        return value.astype(BF16)


    def put(source, parts, target, name, *others):
        return place_rows(after(table, *others), source, routes, parts, target, name)

    outs_ahead = outs_of(1)
    outs_final = swap(outs_ahead, "mp", 2)
    qkv_far = whole_qkv.split(outs_ahead)

    output = put(tokens, [(upd, 0)], None, "put_own", qkv_far)
    ffn_now = ffn.close(output)
    upd_all = [upd] + [swap(after(upd, output), "mp", j) for j in (1, 2)] + [None]
    out_half = outs_of(0, after(outs_final, ffn_now))
    last = call(
        last_pair_body,
        (3,),
        pieces
        + [pl.BlockSpec((routed, width), lambda i, w: (jnp.minimum(i, 1), 0))] * 2
        + [line]
        + [whole((8, width))] * 2
        + [whole((8, 128))] * 2,
        [part],
        [sds((pair + 16, width), BF16)],
        1,
        1,
        "last",
        scratch=[pltpu.VMEM((8, width), F32)],
    )(
        after(table, out_half), back_keep[0], last_first_a, last_final_a, back_keep[1],
        last_first_b, last_final_b, xr_rows, base, gain_attn, gain_two_part, router_part, *score,
    )[0]
    grads = put(cotangent, [(last, 0)], None, "put_own", last)
    qkv_now = whole_qkv.cross(grads)
    upd_all[1:3] = [after(value, qkv_now) for value in upd_all[1:3]]
    last_all = [last] + [swap(after(last, *upd_all[1:3]), "mp", j) for j in (1, 2)] + [None]
    upd_all[3] = swap(upd_all[1], "mp", 2)
    output = put(tokens, [(upd_all[1], 2), (upd_all[2], 4)], output, "put_out", grads)
    last_all[1:3] = [after(value, output) for value in last_all[1:3]]
    last_all[3] = swap(last_all[2], "mp", 1)
    out_sent = swap(after(out_half, *last_all[1:3]), "dp", 2)
    grads = put(cotangent, [(last_all[1], 2), (last_all[2], 4)], grads, "put_grad", qkv_now)
    upd_all[3] = after(upd_all[3], grads)
    output = put(tokens, [(upd_all[3], 6)], output, "put_out", grads)
    out_half = add(out_half, after(out_sent, output))
    out_sent = swap(out_half, "dp", 4)
    qkv_now = whole_qkv.close(out_half)
    ffn.share(qkv_now)
    last_all[3] = after(last_all[3], qkv_now)
    small = 0.0
    for rows in last_all:
        small = small + rows[pair : pair + 8].astype(F32) + rows[pair + 8 :].astype(F32)
    small_sent = swap(small, "dp", 2)
    grads = put(cotangent, [(last_all[3], 6)], grads, "put_grad", small)
    small = small + after(small_sent, grads)
    small_sent = swap(small, "dp", 4)
    side = ffn.back(small)
    ffn.pair = after(ffn.pair, side)
    whole_qkv.share(ffn.pair)
    grad_down, grad_up = join_halves(after(table, side), ffn.pieces())
    side = whole_qkv.back(grad_up)
    whole_qkv.pair = after(whole_qkv.pair, side)
    small = small + after(small_sent, whole_qkv.pair)
    small_sent = swap(small, "dp", 1)
    out_half = add(out_half, after(out_sent, small))
    out_sent = swap(out_half, "dp", 1)
    grad_qkv, grad_out = join_tail(
        after(table, out_half), whole_qkv.pieces(), [out_half, out_sent]
    )
    small = small + after(small_sent, grad_out)

    score_total = small[3, 0]
    routed_total = small[3, 128]
    token_count = seqs * length * lax.axis_size("dp")
    return (
        output,
        grads,
        small[0],
        small[1],
        small[2],
        grad_qkv,
        grad_out,
        grad_up,
        grad_down,
        routed_total / score_total,
        score_total / token_count,
    )


def shards(*arrays):
    tokens, segments, routes, w_out, w_up = (arrays[at] for at in (0, 1, 2, 8, 9))
    square = lax.axis_size("mp") == 4 and segments.shape[0] == 8 and lax.axis_size("dp") == 8
    square = square and w_up.shape[1] == tokens.shape[1] and tokens.shape[1] % 256 == 0
    if square and routes.shape[1] % 128 == 0 and w_out.shape[0] % 128 == 0:
        return paired(*arrays)
    return general(*arrays)


def solution(mesh):
    rows = P("dp", None)
    columns = P(None, "mp")
    lines = P("mp", None)
    in_specs = (rows, rows, rows, rows, P(), P(), P(), columns, lines, columns, lines)
    out_specs = (rows, rows, P(), P(), P(), columns, lines, columns, lines, P(), P())
    return jax.shard_map(shards, mesh=mesh, in_specs=in_specs, out_specs=out_specs, check_vma=False)
```

profile of v0, /device:TPU:0, one launch (start us, length us, event | category | flops | bytes accessed | tf_op | source)
XLA Modules:
  0.0 279.6 jit_solution(9907333309694556135)
XLA Ops:
  0.6 3.0 %collective-permute-start.1 = (bf16[256,1024]{1,0:T(8,128)(2,1)}, bf16[256,1024]{1,0:T(8,128)(2,1)S(1)}, u32[]{:S(2)}, u32[]{:S(2)}) collective-permute-start(bf16[256,1024]{1,0:T(8,128)(2,1)} %refs_12_.5), channel_id=1, source_target_pairs={{0,1},{1,0},{2,3},{3,2},{4,5},{5,4},{6,7},{7,6},{8,9},{9,8},{10,11... | collective-permute-start | bytes 1572872 | tf_op jit(solution)/shard_map/ppermute | solution.py:303
  6.4 10.6 %front.2 = (bf16[2,2,2,128,1024]{4,3,2,1,0:T(8,128)(2,1)}, bf16[2,2,2,128,512]{4,3,2,1,0:T(8,128)(2,1)}, bf16[2,2,2,128,512]{4,3,2,1,0:T(8,128)(2,1)}, bf16[512,...) custom-call(s32[25]{0:T(128)} %compare_select_fusion.4.where, ...), custom_call_target="tpu_custom_call" | custom-call | flops 15600000000 | bytes 1 | tf_op jit(solution)/shard_map/front/pallas_call | solution.py:1184
  17.0 2.0 collective-permute-start
  20.5 10.6 %front.3 = (bf16[2,2,2,128,1024]{4,3,2,1,0:T(8,128)(2,1)}, bf16[2,2,2,128,512]{4,3,2,1,0:T(8,128)(2,1)}, bf16[2,2,2,128,512]{4,3,2,1,0:T(8,128)(2,1)}, bf16[512,...) custom-call(s32[25]{0:T(128)} %compare_select_fusion.4.where, ...), custom_call_target="tpu_custom_call", output_to_operand_aliasing={{0}: (8, {}), {1}: (9, {}), {2}: (10, {})} | custom-call | flops 15600000000 | bytes 1 | tf_op jit(solution)/shard_map/front/pallas_call | solution.py:1184
  32.7 1.8 collective-permute-start.5
  34.7 12.9 %cot.1 = (bf16[1024,1024]{1,0:T(8,128)(2,1)}, bf16[1024,1024]{1,0:T(8,128)(2,1)}, f32[1024,1024]{1,0:T(8,128)}) custom-call(s32[25]{0:T(128)} %compare_select_fusion.4.where, bf16[8192,1024]{1,0:T(8,128)(2,1)} %source.11, bf16[8192,1024]{1,0:T(8,128)(2,1)} %source.11, s32[8,128]{1,0:T(8,128)} %routes.11, bf16[1024,1024]{1,0:T(8,128)(2,1)} %bitcast.43, ...), custom_call_target="tpu_custom_call" | custom-call | flops 19200000000 | bytes 1 | tf_op jit(solution)/shard_map/cot/pallas_call | solution.py:1230
  47.7 1.8 collective-permute-start.6
  50.6 11.4 %middle.2 = (f32[128,1024]{1,0:T(8,128)}, bf16[2,2,2,128,1024]{4,3,2,1,0:T(8,128)(2,1)}, bf16[2,2,2,128,1024]{4,3,2,1,0:T(8,128)(2,1)}, bf16[2,2,2,128,1024]{4,3...) custom-call(s32[25]{0:T(128)} %compare_select_fusion.4.where, ...), custom_call_target="tpu_custom_call" | custom-call | flops 16499999744 | bytes 1 | tf_op jit(solution)/shard_map/middle/pallas_call | solution.py:1280
  62.0 1.8 collective-permute-start.10
  64.6 11.7 %middle.3 = (f32[128,1024]{1,0:T(8,128)}, bf16[2,2,2,128,1024]{4,3,2,1,0:T(8,128)(2,1)}, bf16[2,2,2,128,1024]{4,3,2,1,0:T(8,128)(2,1)}, bf16[2,2,2,128,1024]{4,3...) custom-call(s32[25]{0:T(128)} %compare_select_fusion.4.where, ...), custom_call_target="tpu_custom_call", output_to_operand_aliasing={{1}: (14, {}), {2}: (15, {}), {3}: (16, {}), {4}: (17, {}),... | custom-call | flops 16499999744 | bytes 1 | tf_op jit(solution)/shard_map/middle/pallas_call | solution.py:1280
  77.9 6.1 %convolution_convert_fusion.1 = bf16[1024,1024]{1,0:T(8,128)(2,1)} fusion(bf16[1024,1024]{1,0:T(8,128)(2,1)} %bitcast.55, bf16[1024,1024]{1,0:T(8,128)(2,1)} %bitcast.57), kind=kOutput, calls=%fused_computation.5 | convolution fusion | flops 2148532224 | bytes 6291456 | tf_op jit(solution)/shard_map/dot_general | solution.py:20
  84.0 7.3 %mlp.1 = (bf16[256,1024]{1,0:T(8,128)(2,1)}, bf16[256,1024]{1,0:T(8,128)(2,1)}, bf16[256,1024]{1,0:T(8,128)(2,1)}, bf16[256,1024]{1,0:T(8,128)(2,1)}) custom-call(s32[25]{0:T(128)} %compare_select_fusion.4.where, bf16[1024,1024]{1,0:T(8,128)(2,1)} %bitcast.47, bf16[1024,1024]{1,0:T(8,128)(2,1)} %w_down.1), custom_call_target="tpu_custom_call" | custom-call | flops 60000000 | bytes 1 | tf_op jit(solution)/shard_map/mlp/pallas_call | solution.py:1317
  93.7 1.7 collective-permute-start.13
  95.4 4.6 %convolution_convert_fusion = bf16[1024,1024]{1,0:T(8,128)(2,1)S(1)} fusion(bf16[1024,1024]{1,0:T(8,128)(2,1)} %bitcast.56, bf16[1024,1024]{1,0:T(8,128)(2,1)} %bitcast.58), kind=kOutput, calls=%fused_computation.4 | convolution fusion | flops 2148532224 | bytes 6291456 | tf_op jit(solution)/shard_map/dot_general | solution.py:20
  101.8 1.6 collective-permute-start.12
  104.8 6.5 %rows.1 = (f32[256,1024]{1,0:T(8,128)}, bf16[256,1024]{1,0:T(8,128)(2,1)}, f32[8,1024]{1,0:T(8,128)}, bf16[256,256]{1,0:T(8,128)(2,1)}, bf16[256,256]{1,0:T(8,12...) custom-call(s32[25]{0:T(128)} %compare_select_fusion.4.where, ...), custom_call_target="tpu_custom_call" | custom-call | flops 8400000000 | bytes 1 | tf_op jit(solution)/shard_map/rows/pallas_call | solution.py:1341
  114.9 3.8 %outs.1 = (bf16[4,128,1024]{2,1,0:T(8,128)(2,1)}, bf16[4,128,1024]{2,1,0:T(8,128)(2,1)}) custom-call(s32[25]{0:T(128)} %compare_select_fusion.4.where, bf16[512,256]{1,0:T(8,128)(2,1)} %get-tuple-element.142.refs_0_, bf16[512,256]{1,0:T(8,128)(2,1)} %copy-done.24, bf16[512,256]{1,0:T(8,128)(2,1)} %copy-done.25, bf16[512,256]{1,0:T(8,128)(2,1)} %copy-done.27, ...), custom_call_target="tpu_custom_call" | custom-call | flops 5849999872 | bytes 1 | tf_op jit(solution)/shard_map/outs/pallas_call | solution.py:1363
  121.1 1.9 collective-permute-start.25
  123.0 3.7 %collective-permute-done.12 = bf16[512,1024]{1,0:T(8,128)(2,1)} collective-permute-done((bf16[512,1024]{1,0:T(8,128)(2,1)S(1)}, bf16[512,1024]{1,0:T(8,128)(2,1)}, u32[]{:S(2)}, u32[]{:S(2)}) %collective-permute-start.12) | collective-permute-done | bytes 1048608 | tf_op jit(solution)/shard_map/ppermute | solution.py:303
  126.7 2.2 add_convert_fusion.1
  128.9 2.7 collective-permute-start.28
  131.6 7.7 %back.2 = (bf16[2,2,2,128,768]{4,3,2,1,0:T(8,128)(2,1)}, bf16[2,128,1024]{2,1,0:T(8,128)(2,1)}, bf16[2,128,1024]{2,1,0:T(8,128)(2,1)}) custom-call(s32[25]{0:T(128)} %compare_select_fusion.4.where, bf16[512,768]{1,0:T(8,128)(2,1)} %get-tuple-element.199.qkv, bf16[512,128]{1,0:T(8,128)(2,1)} %get-tuple-element.200.mask, f32[512,128]{1,0:T(8,128)} %get-tuple-element.201.lse, ...), custom_call_target="tpu_custom_call" | custom-call | flops 3000000000 | bytes 1 | tf_op jit(solution)/shard_map/back/pallas_call | solution.py:1385
  139.8 8.1 %back.3 = (bf16[2,2,2,128,768]{4,3,2,1,0:T(8,128)(2,1)}, bf16[2,128,1024]{2,1,0:T(8,128)(2,1)}, bf16[2,128,1024]{2,1,0:T(8,128)(2,1)}) custom-call(s32[25]{0:T(128)} %compare_select_fusion.4.where, bf16[512,768]{1,0:T(8,128)(2,1)} %get-tuple-element.207.qkv, bf16[512,128]{1,0:T(8,128)(2,1)} %get-tuple-element.208.mask, ...), custom_call_target="tpu_custom_call", output_to_operand_aliasing={{0}: (9, {})} | custom-call | flops 3000000000 | bytes 1 | tf_op jit(solution)/shard_map/back/pallas_call | solution.py:1385
  148.0 3.5 %bitcast_convert_fusion.1 = bf16[512,768]{1,0:T(8,128)(2,1)} fusion(bf16[2,2,2,128,512]{4,3,2,1,0:T(8,128)(2,1)S(1)} %copy-done.38, bf16[2,2,2,128,768]{4,3,2,1,0:T(8,128)(2,1)} %get-tuple-element.211), kind=kOutput, calls=%fused_computation.7 | convolution fusion | flops 805699584 | bytes 3407872 | tf_op jit(solution)/shard_map/dot_general | solution.py:20
  153.5 1.9 bitcast_convert_fusion
  155.4 2.0 add_convert_fusion.4
  159.1 4.7 %delta.1 = (bf16[256,1024]{1,0:T(8,128)(2,1)}, f32[256,1024]{1,0:T(8,128)}, f32[8,1024]{1,0:T(8,128)}) custom-call(s32[25]{0:T(128)} %compare_select_fusion.4.where, bf16[256,1024]{1,0:T(8,128)(2,1)} %get-tuple-element.175.refs_0_, bf16[256,1024]{1,0:T(8,128)(2,1)} %collective-permute-done.13.refs_1_, bf16[256,1024]{1,0:T(8,128)(2,1)} %collective-permute-done.24.refs_2_, ...), custom_call_target="tpu_custom_call" | custom-call | flops 30000000 | bytes 1 | tf_op jit(solution)/shard_map/delta/pallas_call | solution.py:1432
  163.8 3.0 %collective-permute-done.23.refs_4_ = bf16[2,128,1024]{2,1,0:T(8,128)(2,1)S(1)} collective-permute-done((bf16[2,128,1024]{2,1,0:T(8,128)(2,1)}, bf16[2,128,1024]{2,1,0:T(8,128)(2,1)S(1)}, u32[]{:S(2)}, u32[]{:S(2)}) %collective-permute-start.23) | collective-permute-done | bytes 524320 | tf_op jit(solution)/shard_map/ppermute | solution.py:303
  168.9 3.6 %collective-permute-done.22 = bf16[2,128,1024]{2,1,0:T(8,128)(2,1)} collective-permute-done((bf16[2,128,1024]{2,1,0:T(8,128)(2,1)}, bf16[2,128,1024]{2,1,0:T(8,128)(2,1)}, u32[]{:S(2)}, u32[]{:S(2)}) %collective-permute-start.22) | collective-permute-done | bytes 524320 | tf_op jit(solution)/shard_map/ppermute | solution.py:303
  172.5 1.9 fusion.5
  174.9 1.9 add_convert_fusion.7
  178.4 6.1 %put_own.2.refs_2_ = bf16[8192,1024]{1,0:T(8,128)(2,1)} custom-call(s32[25]{0:T(128)} %compare_select_fusion.4.where, bf16[8192,1024]{1,0:T(8,128)(2,1)} %source.10, s32[8,128]{1,0:T(8,128)} %routes.11, bf16[256,1024]{1,0:T(8,128)(2,1)} %get-tuple-element.243.refs_0_), custom_call_target="tpu_custom_call" | custom-call | flops 30000000 | bytes 1 | tf_op jit(solution)/shard_map/put_own/pallas_call | solution.py:1009
  185.7 1.6 add_convert_fusion.value
  187.3 1.6 collective-permute-start.32
  190.7 4.2 %last.1.refs_0_ = bf16[272,1024]{1,0:T(8,128)(2,1)} custom-call(s32[25]{0:T(128)} %compare_select_fusion.4.where, bf16[2,128,1024]{2,1,0:T(8,128)(2,1)} %get-tuple-element.203.refs_0_, bf16[2,128,1024]{2,1,0:T(8,128)(2,1)} %copy-done.3, bf16[128,1024]{1,0:T(8,128)(2,1)} %collective-permute-done.29.refs_2_, bf16[2,128,1024]{2,1,0:T(8,128)(2,1)} %get-tuple-element.215.refs_3_, ...), custom_call_target="tpu_custom_call" | custom-call | flops 1484999936 | bytes 1 | tf_op jit(solution)/shard_map/last/pallas_call | solution.py:1467
  194.9 6.6 %put_own.3.refs_2_ = bf16[8192,1024]{1,0:T(8,128)(2,1)} custom-call(s32[25]{0:T(128)} %compare_select_fusion.4.where, bf16[8192,1024]{1,0:T(8,128)(2,1)} %source.11, s32[8,128]{1,0:T(8,128)} %routes.11, bf16[272,1024]{1,0:T(8,128)(2,1)} %last.1.refs_0_), custom_call_target="tpu_custom_call" | custom-call | flops 30000000 | bytes 1 | tf_op jit(solution)/shard_map/put_own/pallas_call | solution.py:1009
  204.4 1.6 collective-permute-start.35
  206.1 10.1 %put_out.2.refs_1_ = bf16[8192,1024]{1,0:T(8,128)(2,1)} custom-call(s32[25]{0:T(128)} %compare_select_fusion.4.where, bf16[8192,1024]{1,0:T(8,128)(2,1)} %source.10, s32[8,128]{1,0:T(8,128)} %routes.11, bf16[256,1024]{1,0:T(8,128)(2,1)} %collective-permute-done.31.refs_0_, ...), custom_call_target="tpu_custom_call", output_to_operand_aliasing={{}: (5, {})} | custom-call | flops 14400000000 | bytes 1 | tf_op jit(solution)/shard_map/put_out/pallas_call | solution.py:1009
  216.1 3.5 %collective-permute-done.34.refs_1_ = bf16[272,1024]{1,0:T(8,128)(2,1)} collective-permute-done((bf16[272,1024]{1,0:T(8,128)(2,1)S(1)}, bf16[272,1024]{1,0:T(8,128)(2,1)}, u32[]{:S(2)}, u32[]{:S(2)}) %collective-permute-start.34) | collective-permute-done | bytes 557088 | tf_op jit(solution)/shard_map/ppermute | solution.py:303
  220.9 10.0 %put_grad.2.refs_1_ = bf16[8192,1024]{1,0:T(8,128)(2,1)} custom-call(s32[25]{0:T(128)} %compare_select_fusion.4.where, bf16[8192,1024]{1,0:T(8,128)(2,1)} %source.11, s32[8,128]{1,0:T(8,128)} %routes.11, bf16[272,1024]{1,0:T(8,128)(2,1)} %collective-permute-done.33.refs_0_, ...), custom_call_target="tpu_custom_call", output_to_operand_aliasing={{}: (5, {})} | custom-call | flops 14400000000 | bytes 1 | tf_op jit(solution)/shard_map/put_grad/pallas_call | solution.py:1009
  230.9 1.6 collective-permute-start.38
  232.5 6.1 %put_out.3 = bf16[8192,1024]{1,0:T(8,128)(2,1)} custom-call(s32[25]{0:T(128)} %compare_select_fusion.4.where, bf16[8192,1024]{1,0:T(8,128)(2,1)} %source.10, s32[8,128]{1,0:T(8,128)} %routes.11, bf16[256,1024]{1,0:T(8,128)(2,1)} %collective-permute-done.35.refs_0_, bf16[8192,1024]{1,0:T(8,128)(2,1)} %put_out.2.refs_1_), custom_call_target="tpu_custom_call", output_to_operand_aliasing={{}: (4, {})} | custom-call | flops 7200000000 | bytes 1 | tf_op jit(solution)/shard_map/put_out/pallas_call | solution.py:1009
  238.6 1.9 add_convert_fusion.5.refs_0_
  242.0 6.1 %put_grad.3 = bf16[8192,1024]{1,0:T(8,128)(2,1)} custom-call(s32[25]{0:T(128)} %compare_select_fusion.4.where, bf16[8192,1024]{1,0:T(8,128)(2,1)} %source.11, s32[8,128]{1,0:T(8,128)} %routes.11, bf16[272,1024]{1,0:T(8,128)(2,1)} %copy-done.10, bf16[8192,1024]{1,0:T(8,128)(2,1)} %put_grad.2.refs_1_), custom_call_target="tpu_custom_call", output_to_operand_aliasing={{}: (4, {})} | custom-call | flops 7200000000 | bytes 1 | tf_op jit(solution)/shard_map/put_grad/pallas_call | solution.py:1009
  249.9 2.6 collective-permute-start.47
  253.8 7.0 %join.2 = (f32[1024,1024]{1,0:T(8,128)}, f32[1024,1024]{1,0:T(8,128)}) custom-call(s32[25]{0:T(128)} %compare_select_fusion.4.where, bf16[512,1024]{1,0:T(8,128)(2,1)} %copy-done.6, bf16[512,1024]{1,0:T(8,128)(2,1)} %collective-permute-done.42.side, bf16[512,1024]{1,0:T(8,128)(2,1)} %collective-permute-done.41.pair, bf16[512,1024]{1,0:T(8,128)(2,1)} %copy-done.17), custom_call_target="tpu_custom_call" | custom-call | flops 8999999488 | bytes 1 | tf_op jit(solution)/shard_map/join/pallas_call | solution.py:1040
  260.8 5.1 %collective-permute-done.44.refs_2_ = bf16[256,768]{1,0:T(8,128)(2,1)S(1)} collective-permute-done((bf16[256,768]{1,0:T(8,128)(2,1)S(1)}, bf16[256,768]{1,0:T(8,128)(2,1)S(1)}, u32[]{:S(2)}, u32[]{:S(2)}) %collective-permute-start.44) | collective-permute-done | bytes 393248 | tf_op jit(solution)/shard_map/ppermute | solution.py:303
  269.5 4.7 %join.3 = (f32[1024,768]{1,0:T(8,128)}, f32[256,1024]{1,0:T(8,128)}) custom-call(s32[25]{0:T(128)} %compare_select_fusion.4.where, bf16[256,768]{1,0:T(8,128)(2,1)} %add_convert_fusion.5.refs_0_, bf16[256,768]{1,0:T(8,128)(2,1)} %copy-done.22, bf16[256,768]{1,0:T(8,128)(2,1)} %copy-done.21, bf16[256,768]{1,0:T(8,128)(2,1)} %copy-done.23, ...), custom_call_target="tpu_custom_call" | custom-call | flops 8999999488 | bytes 1 | tf_op jit(solution)/shard_map/join/pallas_call | solution.py:1066
  (178 shorter events, 45.9 us)
Async XLA Ops:
  0.6 30.5 %collective-permute-start.1 = (bf16[256,1024]{1,0:T(8,128)(2,1)}, bf16[256,1024]{1,0:T(8,128)(2,1)S(1)}, u32[]{:S(2)}, u32[]{:S(2)}) collective-permute-start(bf16[256,1024]{1,0:T(8,128)(2,1)} %refs_12_.5), channel_id=1, source_target_pairs={{0,1},{1,0},{2,3},{3,2},{4,5},{5,4},{6,7},{7,6},{8,9},{9,8},{10,11... | collective-permute-start | bytes 1572872 | tf_op jit(solution)/shard_map/ppermute | solution.py:303
  3.7 27.5 %collective-permute-start.2 = (bf16[256,1024]{1,0:T(8,128)(2,1)}, bf16[256,1024]{1,0:T(8,128)(2,1)S(1)}, u32[]{:S(2)}, u32[]{:S(2)}) collective-permute-start(bf16[256,1024]{1,0:T(8,128)(2,1)} %refs_12_.5), channel_id=1, source_target_pairs={{0,2},{1,3},{2,0},{3,1},{4,6},{5,7},{6,4},{7,5},{8,10},{9,11},{10,... | collective-permute-start | bytes 1572872 | tf_op jit(solution)/shard_map/ppermute | solution.py:303
  5.2 26.0 %collective-permute-start.3 = (bf16[256,1024]{1,0:T(8,128)(2,1)}, bf16[256,1024]{1,0:T(8,128)(2,1)S(1)}, u32[]{:S(2)}, u32[]{:S(2)}) collective-permute-start(bf16[256,1024]{1,0:T(8,128)(2,1)} %refs_12_.5), channel_id=1, source_target_pairs={{0,3},{1,2},{2,1},{3,0},{4,7},{5,6},{6,5},{7,4},{8,11},{9,10},{10,... | collective-permute-start | bytes 1572872 | tf_op jit(solution)/shard_map/ppermute | solution.py:303
  17.0 15.7 %collective-permute-start = (bf16[512,256]{1,0:T(8,128)(2,1)}, bf16[512,256]{1,0:T(8,128)(2,1)S(1)}, u32[]{:S(2)}, u32[]{:S(2)}) collective-permute-start(bf16[512,256]{1,0:T(8,128)(2,1)} %get-tuple-element.142.refs_0_), channel_id=1, source_target_pairs={{0,1},{1,0},{2,3},{3,2},{4,5},{5,4},{6,7},{7,6},{8,9},{9,8},{10,11... | collective-permute-start | bytes 786440 | tf_op jit(solution)/shard_map/ppermute | solution.py:303
  19.0 30.8 %collective-permute-start.4 = (bf16[512,256]{1,0:T(8,128)(2,1)}, bf16[512,256]{1,0:T(8,128)(2,1)S(1)}, u32[]{:S(2)}, u32[]{:S(2)}) collective-permute-start(bf16[512,256]{1,0:T(8,128)(2,1)} %get-tuple-element.142.refs_0_), channel_id=1, source_target_pairs={{0,2},{1,3},{2,0},{3,1},{4,6},{5,7},{6,4},{7,5},{8,10},{9,11},{10,... | collective-permute-start | bytes 786440 | tf_op jit(solution)/shard_map/ppermute | solution.py:303
  32.7 17.1 %collective-permute-start.5 = (bf16[512,256]{1,0:T(8,128)(2,1)S(1)}, bf16[512,256]{1,0:T(8,128)(2,1)S(1)}, u32[]{:S(2)}, u32[]{:S(2)}) collective-permute-start(bf16[512,256]{1,0:T(8,128)(2,1)S(1)} %collective-permute-done.refs_1_), channel_id=1, source_target_pairs={{0,2},{1,3},{2,0},{3,1},{4,6},{5,7},{6,4},{7,5},{8,10},{9,11},{10,... | collective-permute-start | bytes 786440 | tf_op jit(solution)/shard_map/ppermute | solution.py:303
  34.5 15.0 %collective-permute-start.7 = (bf16[512,256]{1,0:T(8,128)(2,1)}, bf16[512,256]{1,0:T(8,128)(2,1)S(1)}, u32[]{:S(2)}, u32[]{:S(2)}) collective-permute-start(bf16[512,256]{1,0:T(8,128)(2,1)} %get-tuple-element.158.refs_0_.refs_4_), channel_id=1, source_target_pairs={{0,2},{1,3},{2,0},{3,1},{4,6},{5,7},{6,4},{7,5},{8,10},{9,11},{10,... | collective-permute-start | bytes 786440 | tf_op jit(solution)/shard_map/ppermute | solution.py:303
  47.7 16.1 %collective-permute-start.6 = (bf16[512,256]{1,0:T(8,128)(2,1)S(1)}, bf16[512,256]{1,0:T(8,128)(2,1)S(1)}, u32[]{:S(2)}, u32[]{:S(2)}) collective-permute-start(bf16[512,256]{1,0:T(8,128)(2,1)S(1)} %copy-done.26), channel_id=1, source_target_pairs={{0,1},{1,0},{2,3},{3,2},{4,5},{5,4},{6,7},{7,6},{8,9},{9,8},{10,11... | collective-permute-start | bytes 786440 | tf_op jit(solution)/shard_map/ppermute | solution.py:303
  49.5 14.3 %collective-permute-start.8 = (bf16[512,256]{1,0:T(8,128)(2,1)S(1)}, bf16[512,256]{1,0:T(8,128)(2,1)S(1)}, u32[]{:S(2)}, u32[]{:S(2)}) collective-permute-start(bf16[512,256]{1,0:T(8,128)(2,1)S(1)} %collective-permute-done.7.refs_2_.refs_6_), channel_id=1, source_target_pairs={{0,1},{1,0},{2,3},{3,2},{4,5},{5,4},{6,7},{7,6},{8,9},{9,8},{10,11... | collective-permute-start | bytes 786440 | tf_op jit(solution)/shard_map/ppermute | solution.py:303
  62.0 15.9 %collective-permute-start.10 = (bf16[2,128,1024]{2,1,0:T(8,128)(2,1)}, bf16[2,128,1024]{2,1,0:T(8,128)(2,1)S(1)}, u32[]{:S(2)}, u32[]{:S(2)}) collective-permute-start(bf16[2,128,1024]{2,1,0:T(8,128)(2,1)} %get-tuple-element.169), channel_id=1, source_target_pairs={{0,1},{1,0},{2,3},{3,2},{4,5},{5,4},{6,7},{7,6},{8,9},{9,8},{10,11... | collective-permute-start | bytes 1572872 | tf_op jit(solution)/shard_map/ppermute | solution.py:303
  76.3 15.1 %collective-permute-start.9 = (bf16[2,128,1024]{2,1,0:T(8,128)(2,1)}, bf16[2,128,1024]{2,1,0:T(8,128)(2,1)S(1)}, u32[]{:S(2)}, u32[]{:S(2)}) collective-permute-start(bf16[2,128,1024]{2,1,0:T(8,128)(2,1)} %get-tuple-element.167), channel_id=1, source_target_pairs={{0,2},{1,3},{2,0},{3,1},{4,6},{5,7},{6,4},{7,5},{8,10},{9,11},{10,... | collective-permute-start | bytes 1572872 | tf_op jit(solution)/shard_map/ppermute | solution.py:303
  92.9 7.2 %collective-permute-start.11 = (bf16[1024,1024]{1,0:T(8,128)(2,1)}, bf16[1024,1024]{1,0:T(8,128)(2,1)S(1)}, u32[]{:S(2)}, u32[]{:S(2)}) collective-permute-start(bf16[1024,1024]{1,0:T(8,128)(2,1)} %convolution_convert_fusion.1), channel_id=1, source_target_pairs={{0,4},{4,0},{8,12},{12,8},{16,20},{20,16},{24,28},{28,24},{1,5},{5... | collective-permute-start | bytes 6291464 | tf_op jit(solution)/shard_map/ppermute | solution.py:303
  92.9 10.5 %collective-permute-start.14 = (bf16[128,1024]{1,0:T(8,128)(2,1)S(1)}, bf16[128,1024]{1,0:T(8,128)(2,1)S(1)}, u32[]{:S(2)}, u32[]{:S(2)}) collective-permute-start(bf16[128,1024]{1,0:T(8,128)(2,1)S(1)} %fusion.1), channel_id=1, source_target_pairs={{0,2},{1,3},{2,0},{3,1},{4,6},{5,7},{6,4},{7,5},{8,10},{9,11},{10,... | collective-permute-start | bytes 786440 | tf_op jit(solution)/shard_map/ppermute | solution.py:303
  93.4 10.7 %collective-permute-start.15 = (bf16[128,1024]{1,0:T(8,128)(2,1)}, bf16[128,1024]{1,0:T(8,128)(2,1)S(1)}, u32[]{:S(2)}, u32[]{:S(2)}) collective-permute-start(bf16[128,1024]{1,0:T(8,128)(2,1)} %fusion.2), channel_id=1, source_target_pairs={{0,1},{1,0},{2,3},{3,2},{4,5},{5,4},{6,7},{7,6},{8,9},{9,8},{10,11... | collective-permute-start | bytes 786440 | tf_op jit(solution)/shard_map/ppermute | solution.py:303
  93.7 26.5 %collective-permute-start.13 = (bf16[256,1024]{1,0:T(8,128)(2,1)}, bf16[256,1024]{1,0:T(8,128)(2,1)}, u32[]{:S(2)}, u32[]{:S(2)}) collective-permute-start(bf16[256,1024]{1,0:T(8,128)(2,1)} %get-tuple-element.182), channel_id=1, source_target_pairs={{0,1},{1,0},{2,3},{3,2},{4,5},{5,4},{6,7},{7,6},{8,9},{9,8},{10,11... | collective-permute-start | bytes 1572872 | tf_op jit(solution)/shard_map/ppermute | solution.py:303
  101.8 24.9 %collective-permute-start.12 = (bf16[512,1024]{1,0:T(8,128)(2,1)S(1)}, bf16[512,1024]{1,0:T(8,128)(2,1)}, u32[]{:S(2)}, u32[]{:S(2)}) collective-permute-start(bf16[512,1024]{1,0:T(8,128)(2,1)S(1)} %add_convert_fusion.2), channel_id=1, source_target_pairs={{0,8},{4,12},{8,0},{12,4},{16,24},{20,28},{24,16},{28,20},{1,9},{5... | collective-permute-start | bytes 3145736 | tf_op jit(solution)/shard_map/ppermute | solution.py:303
  111.4 7.3 %collective-permute-start.16 = (bf16[256,256]{1,0:T(8,128)(2,1)}, bf16[256,256]{1,0:T(8,128)(2,1)S(1)}, u32[]{:S(2)}, u32[]{:S(2)}) collective-permute-start(bf16[256,256]{1,0:T(8,128)(2,1)} %get-tuple-element.187), channel_id=1, source_target_pairs={{0,1},{1,0},{2,3},{3,2},{4,5},{5,4},{6,7},{7,6},{8,9},{9,8},{10,11... | collective-permute-start | bytes 393224 | tf_op jit(solution)/shard_map/ppermute | solution.py:303
  112.0 6.8 %collective-permute-start.17 = (bf16[256,256]{1,0:T(8,128)(2,1)}, bf16[256,256]{1,0:T(8,128)(2,1)S(1)}, u32[]{:S(2)}, u32[]{:S(2)}) collective-permute-start(bf16[256,256]{1,0:T(8,128)(2,1)} %get-tuple-element.192), channel_id=1, source_target_pairs={{0,2},{1,3},{2,0},{3,1},{4,6},{5,7},{6,4},{7,5},{8,10},{9,11},{10,... | collective-permute-start | bytes 393224 | tf_op jit(solution)/shard_map/ppermute | solution.py:303
  113.5 6.7 %collective-permute-start.18 = (bf16[256,256]{1,0:T(8,128)(2,1)}, bf16[256,256]{1,0:T(8,128)(2,1)S(1)}, u32[]{:S(2)}, u32[]{:S(2)}) collective-permute-start(bf16[256,256]{1,0:T(8,128)(2,1)} %get-tuple-element.194), channel_id=1, source_target_pairs={{0,3},{1,2},{2,1},{3,0},{4,7},{5,6},{6,5},{7,4},{8,11},{9,10},{10,... | collective-permute-start | bytes 393224 | tf_op jit(solution)/shard_map/ppermute | solution.py:303
  118.7 32.7 %collective-permute-start.21 = (bf16[4,128,1024]{2,1,0:T(8,128)(2,1)}, bf16[4,128,1024]{2,1,0:T(8,128)(2,1)}, u32[]{:S(2)}, u32[]{:S(2)}) collective-permute-start(bf16[4,128,1024]{2,1,0:T(8,128)(2,1)} %get-tuple-element.214), channel_id=1, source_target_pairs={{0,4},{4,0},{8,12},{12,8},{16,20},{20,16},{24,28},{28,24},{1,5},{5... | collective-permute-start | bytes 3145736 | tf_op jit(solution)/shard_map/ppermute | solution.py:303
  120.2 37.2 %collective-permute-start.24 = (bf16[256,1024]{1,0:T(8,128)(2,1)}, bf16[256,1024]{1,0:T(8,128)(2,1)}, u32[]{:S(2)}, u32[]{:S(2)}) collective-permute-start(bf16[256,1024]{1,0:T(8,128)(2,1)} %get-tuple-element.221), channel_id=1, source_target_pairs={{0,2},{1,3},{2,0},{3,1},{4,6},{5,7},{6,4},{7,5},{8,10},{9,11},{10,... | collective-permute-start | bytes 1572872 | tf_op jit(solution)/shard_map/ppermute | solution.py:303
  121.1 37.5 %collective-permute-start.25 = (bf16[256,1024]{1,0:T(8,128)(2,1)}, bf16[256,1024]{1,0:T(8,128)(2,1)}, u32[]{:S(2)}, u32[]{:S(2)}) collective-permute-start(bf16[256,1024]{1,0:T(8,128)(2,1)} %get-tuple-element.224), channel_id=1, source_target_pairs={{0,3},{1,2},{2,1},{3,0},{4,7},{5,6},{6,5},{7,4},{8,11},{9,10},{10,... | collective-permute-start | bytes 1572872 | tf_op jit(solution)/shard_map/ppermute | solution.py:303
  128.9 55.6 %collective-permute-start.28 = (bf16[512,1024]{1,0:T(8,128)(2,1)S(1)}, bf16[512,1024]{1,0:T(8,128)(2,1)}, u32[]{:S(2)}, u32[]{:S(2)}) collective-permute-start(bf16[512,1024]{1,0:T(8,128)(2,1)S(1)} %add_convert_fusion.1), channel_id=1, source_target_pairs={{0,16},{4,20},{8,24},{12,28},{16,0},{20,4},{24,8},{28,12},{1,17},{... | collective-permute-start | bytes 3145736 | tf_op jit(solution)/shard_map/ppermute | solution.py:303
  139.3 12.6 %collective-permute-start.19 = (bf16[2,128,1024]{2,1,0:T(8,128)(2,1)}, bf16[2,128,1024]{2,1,0:T(8,128)(2,1)S(1)}, u32[]{:S(2)}, u32[]{:S(2)}) collective-permute-start(bf16[2,128,1024]{2,1,0:T(8,128)(2,1)} %get-tuple-element.204), channel_id=1, source_target_pairs={{0,1},{1,0},{2,3},{3,2},{4,5},{5,4},{6,7},{7,6},{8,9},{9,8},{10,11... | collective-permute-start | bytes 1572872 | tf_op jit(solution)/shard_map/ppermute | solution.py:303
  151.4 23.5 %collective-permute-start.20 = (bf16[512,768]{1,0:T(8,128)(2,1)}, bf16[512,768]{1,0:T(8,128)(2,1)}, u32[]{:S(2)}, u32[]{:S(2)}) collective-permute-start(bf16[512,768]{1,0:T(8,128)(2,1)} %bitcast_convert_fusion.1), channel_id=1, source_target_pairs={{0,4},{4,0},{8,12},{12,8},{16,20},{20,16},{24,28},{28,24},{1,5},{5... | collective-permute-start | bytes 2359304 | tf_op jit(solution)/shard_map/ppermute | solution.py:303
  151.9 15.0 %collective-permute-start.23 = (bf16[2,128,1024]{2,1,0:T(8,128)(2,1)}, bf16[2,128,1024]{2,1,0:T(8,128)(2,1)S(1)}, u32[]{:S(2)}, u32[]{:S(2)}) collective-permute-start(bf16[2,128,1024]{2,1,0:T(8,128)(2,1)} %get-tuple-element.218), channel_id=1, source_target_pairs={{0,2},{1,3},{2,0},{3,1},{4,6},{5,7},{6,4},{7,5},{8,10},{9,11},{10,... | collective-permute-start | bytes 1572872 | tf_op jit(solution)/shard_map/ppermute | solution.py:303
  157.4 15.1 %collective-permute-start.22 = (bf16[2,128,1024]{2,1,0:T(8,128)(2,1)}, bf16[2,128,1024]{2,1,0:T(8,128)(2,1)}, u32[]{:S(2)}, u32[]{:S(2)}) collective-permute-start(bf16[2,128,1024]{2,1,0:T(8,128)(2,1)} %add_convert_fusion.4), channel_id=1, source_target_pairs={{0,1},{1,0},{2,3},{3,2},{4,5},{5,4},{6,7},{7,6},{8,9},{9,8},{10,11... | collective-permute-start | bytes 1572872 | tf_op jit(solution)/shard_map/ppermute | solution.py:303
  158.6 31.6 %collective-permute-start.29 = (bf16[128,1024]{1,0:T(8,128)(2,1)S(1)}, bf16[128,1024]{1,0:T(8,128)(2,1)}, u32[]{:S(2)}, u32[]{:S(2)}) collective-permute-start(bf16[128,1024]{1,0:T(8,128)(2,1)S(1)} %fusion.3), channel_id=1, source_target_pairs={{0,2},{1,3},{2,0},{3,1},{4,6},{5,7},{6,4},{7,5},{8,10},{9,11},{10,... | collective-permute-start | bytes 786440 | tf_op jit(solution)/shard_map/ppermute | solution.py:303
  167.8 23.0 %collective-permute-start.30 = (bf16[128,1024]{1,0:T(8,128)(2,1)}, bf16[128,1024]{1,0:T(8,128)(2,1)}, u32[]{:S(2)}, u32[]{:S(2)}) collective-permute-start(bf16[128,1024]{1,0:T(8,128)(2,1)} %fusion.4), channel_id=1, source_target_pairs={{0,1},{1,0},{2,3},{3,2},{4,5},{5,4},{6,7},{7,6},{8,9},{9,8},{10,11... | collective-permute-start | bytes 786440 | tf_op jit(solution)/shard_map/ppermute | solution.py:303
  174.4 12.9 %collective-permute-start.27 = (bf16[128,1024]{1,0:T(8,128)(2,1)}, bf16[128,1024]{1,0:T(8,128)(2,1)}, u32[]{:S(2)}, u32[]{:S(2)}) collective-permute-start(bf16[128,1024]{1,0:T(8,128)(2,1)} %fusion.5), channel_id=1, source_target_pairs={{0,2},{1,3},{2,0},{3,1},{4,6},{5,7},{6,4},{7,5},{8,10},{9,11},{10,... | collective-permute-start | bytes 786440 | tf_op jit(solution)/shard_map/ppermute | solution.py:303
  176.8 24.7 %collective-permute-start.26 = (bf16[256,768]{1,0:T(8,128)(2,1)}, bf16[256,768]{1,0:T(8,128)(2,1)}, u32[]{:S(2)}, u32[]{:S(2)}) collective-permute-start(bf16[256,768]{1,0:T(8,128)(2,1)} %add_convert_fusion.7), channel_id=1, source_target_pairs={{0,8},{4,12},{8,0},{12,4},{16,24},{20,28},{24,16},{28,20},{1,9},{5... | collective-permute-start | bytes 1179656 | tf_op jit(solution)/shard_map/ppermute | solution.py:303
  184.4 18.7 %collective-permute-start.31 = (bf16[256,1024]{1,0:T(8,128)(2,1)}, bf16[256,1024]{1,0:T(8,128)(2,1)}, u32[]{:S(2)}, u32[]{:S(2)}) collective-permute-start(bf16[256,1024]{1,0:T(8,128)(2,1)} %get-tuple-element.243.refs_0_), channel_id=1, source_target_pairs={{0,1},{1,0},{2,3},{3,2},{4,5},{5,4},{6,7},{7,6},{8,9},{9,8},{10,11... | collective-permute-start | bytes 1572872 | tf_op jit(solution)/shard_map/ppermute | solution.py:303
  187.3 15.9 %collective-permute-start.32 = (bf16[256,1024]{1,0:T(8,128)(2,1)}, bf16[256,1024]{1,0:T(8,128)(2,1)}, u32[]{:S(2)}, u32[]{:S(2)}) collective-permute-start(bf16[256,1024]{1,0:T(8,128)(2,1)} %get-tuple-element.243.refs_0_), channel_id=1, source_target_pairs={{0,2},{1,3},{2,0},{3,1},{4,6},{5,7},{6,4},{7,5},{8,10},{9,11},{10,... | collective-permute-start | bytes 1572872 | tf_op jit(solution)/shard_map/ppermute | solution.py:303
  190.2 57.8 %collective-permute-start.42 = (bf16[512,1024]{1,0:T(8,128)(2,1)S(1)}, bf16[512,1024]{1,0:T(8,128)(2,1)}, u32[]{:S(2)}, u32[]{:S(2)}) collective-permute-start(bf16[512,1024]{1,0:T(8,128)(2,1)S(1)} %add_convert_fusion.value), channel_id=1, source_target_pairs={{0,8},{4,12},{8,0},{12,4},{16,24},{20,28},{24,16},{28,20},{1,9},{5... | collective-permute-start | bytes 3145736 | tf_op jit(solution)/shard_map/ppermute | solution.py:303
  202.8 35.8 %collective-permute-start.37 = (bf16[256,768]{1,0:T(8,128)(2,1)S(1)}, bf16[256,768]{1,0:T(8,128)(2,1)}, u32[]{:S(2)}, u32[]{:S(2)}) collective-permute-start(bf16[256,768]{1,0:T(8,128)(2,1)S(1)} %add_convert_fusion.6), channel_id=1, source_target_pairs={{0,16},{4,20},{8,24},{12,28},{16,0},{20,4},{24,8},{28,12},{1,17},{... | collective-permute-start | bytes 1179656 | tf_op jit(solution)/shard_map/ppermute | solution.py:303
  203.2 12.9 %collective-permute-start.33 = (bf16[272,1024]{1,0:T(8,128)(2,1)S(1)}, bf16[272,1024]{1,0:T(8,128)(2,1)}, u32[]{:S(2)}, u32[]{:S(2)}) collective-permute-start(bf16[272,1024]{1,0:T(8,128)(2,1)S(1)} %copy-done), channel_id=1, source_target_pairs={{0,1},{1,0},{2,3},{3,2},{4,5},{5,4},{6,7},{7,6},{8,9},{9,8},{10,11... | collective-permute-start | bytes 1671176 | tf_op jit(solution)/shard_map/ppermute | solution.py:303
  204.0 15.6 %collective-permute-start.34 = (bf16[272,1024]{1,0:T(8,128)(2,1)S(1)}, bf16[272,1024]{1,0:T(8,128)(2,1)}, u32[]{:S(2)}, u32[]{:S(2)}) collective-permute-start(bf16[272,1024]{1,0:T(8,128)(2,1)S(1)} %copy-done), channel_id=1, source_target_pairs={{0,2},{1,3},{2,0},{3,1},{4,6},{5,7},{6,4},{7,5},{8,10},{9,11},{10,... | collective-permute-start | bytes 1671176 | tf_op jit(solution)/shard_map/ppermute | solution.py:303
  204.4 26.5 %collective-permute-start.35 = (bf16[256,1024]{1,0:T(8,128)(2,1)}, bf16[256,1024]{1,0:T(8,128)(2,1)}, u32[]{:S(2)}, u32[]{:S(2)}) collective-permute-start(bf16[256,1024]{1,0:T(8,128)(2,1)} %collective-permute-done.31.refs_0_), channel_id=1, source_target_pairs={{0,2},{1,3},{2,0},{3,1},{4,6},{5,7},{6,4},{7,5},{8,10},{9,11},{10,... | collective-permute-start | bytes 1572872 | tf_op jit(solution)/shard_map/ppermute | solution.py:303
  219.6 20.8 %collective-permute-start.36 = (bf16[272,1024]{1,0:T(8,128)(2,1)}, bf16[272,1024]{1,0:T(8,128)(2,1)S(1)}, u32[]{:S(2)}, u32[]{:S(2)}) collective-permute-start(bf16[272,1024]{1,0:T(8,128)(2,1)} %collective-permute-done.34.refs_1_), channel_id=1, source_target_pairs={{0,1},{1,0},{2,3},{3,2},{4,5},{5,4},{6,7},{7,6},{8,9},{9,8},{10,11... | collective-permute-start | bytes 1671176 | tf_op jit(solution)/shard_map/ppermute | solution.py:303
  230.9 7.6 %collective-permute-start.38 = (bf16[128,1024]{1,0:T(8,128)(2,1)S(1)}, bf16[128,1024]{1,0:T(8,128)(2,1)S(1)}, u32[]{:S(2)}, u32[]{:S(2)}) collective-permute-start(bf16[128,1024]{1,0:T(8,128)(2,1)S(1)} %fusion), channel_id=1, source_target_pairs={{0,8},{4,12},{8,0},{12,4},{16,24},{20,28},{24,16},{28,20},{1,9},{5... | collective-permute-start | bytes 786440 | tf_op jit(solution)/shard_map/ppermute | solution.py:303
  240.5 12.3 %collective-permute-start.41 = (bf16[512,1024]{1,0:T(8,128)(2,1)S(1)}, bf16[512,1024]{1,0:T(8,128)(2,1)}, u32[]{:S(2)}, u32[]{:S(2)}) collective-permute-start(bf16[512,1024]{1,0:T(8,128)(2,1)S(1)} %add_convert_fusion.value), channel_id=1, source_target_pairs={{0,4},{4,0},{8,12},{12,8},{16,20},{20,16},{24,28},{28,24},{1,5},{5... | collective-permute-start | bytes 3145736 | tf_op jit(solution)/shard_map/ppermute | solution.py:303
  241.4 6.6 %collective-permute-start.39 = (f32[8,1024]{1,0:T(8,128)S(1)}, f32[8,1024]{1,0:T(8,128)S(1)}, u32[]{:S(2)}, u32[]{:S(2)}) collective-permute-start(f32[8,1024]{1,0:T(8,128)S(1)} %convert_add_fusion), channel_id=1, source_target_pairs={{0,8},{4,12},{8,0},{12,4},{16,24},{20,28},{24,16},{28,20},{1,9},{5... | collective-permute-start | bytes 98312 | tf_op jit(solution)/shard_map/ppermute | solution.py:303
  248.0 4.8 %collective-permute-start.45 = (bf16[512,1024]{1,0:T(8,128)(2,1)}, bf16[512,1024]{1,0:T(8,128)(2,1)S(1)}, u32[]{:S(2)}, u32[]{:S(2)}) collective-permute-start(bf16[512,1024]{1,0:T(8,128)(2,1)} %collective-permute-done.42.side), channel_id=1, source_target_pairs={{0,4},{4,0},{8,12},{12,8},{16,20},{20,16},{24,28},{28,24},{1,5},{5... | collective-permute-start | bytes 3145736 | tf_op jit(solution)/shard_map/ppermute | solution.py:303
  248.3 17.7 %collective-permute-start.44 = (bf16[256,768]{1,0:T(8,128)(2,1)S(1)}, bf16[256,768]{1,0:T(8,128)(2,1)S(1)}, u32[]{:S(2)}, u32[]{:S(2)}) collective-permute-start(bf16[256,768]{1,0:T(8,128)(2,1)S(1)} %copy-done.11), channel_id=1, source_target_pairs={{0,8},{4,12},{8,0},{12,4},{16,24},{20,28},{24,16},{28,20},{1,9},{5... | collective-permute-start | bytes 1179656 | tf_op jit(solution)/shard_map/ppermute | solution.py:303
  249.9 16.1 %collective-permute-start.47 = (bf16[128,1024]{1,0:T(8,128)(2,1)S(1)}, bf16[128,1024]{1,0:T(8,128)(2,1)S(1)}, u32[]{:S(2)}, u32[]{:S(2)}) collective-permute-start(bf16[128,1024]{1,0:T(8,128)(2,1)S(1)} %add_convert_fusion.10), channel_id=1, source_target_pairs={{0,16},{4,20},{8,24},{12,28},{16,0},{20,4},{24,8},{28,12},{1,17},{... | collective-permute-start | bytes 786440 | tf_op jit(solution)/shard_map/ppermute | solution.py:303
  252.5 13.5 %collective-permute-start.40 = (f32[8,1024]{1,0:T(8,128)S(1)}, f32[8,1024]{1,0:T(8,128)S(1)}, u32[]{:S(2)}, u32[]{:S(2)}) collective-permute-start(f32[8,1024]{1,0:T(8,128)S(1)} %add.174), channel_id=1, source_target_pairs={{0,16},{4,20},{8,24},{12,28},{16,0},{20,4},{24,8},{28,12},{1,17},{... | collective-permute-start | bytes 98312 | tf_op jit(solution)/shard_map/ppermute | solution.py:303
  252.8 13.2 %collective-permute-start.43 = (bf16[256,768]{1,0:T(8,128)(2,1)S(1)}, bf16[256,768]{1,0:T(8,128)(2,1)S(1)}, u32[]{:S(2)}, u32[]{:S(2)}) collective-permute-start(bf16[256,768]{1,0:T(8,128)(2,1)S(1)} %copy-done.11), channel_id=1, source_target_pairs={{0,4},{4,0},{8,12},{12,8},{16,20},{20,16},{24,28},{28,24},{1,5},{5... | collective-permute-start | bytes 1179656 | tf_op jit(solution)/shard_map/ppermute | solution.py:303
  266.7 7.6 %collective-permute-start.46 = (f32[8,1024]{1,0:T(8,128)S(1)}, f32[8,1024]{1,0:T(8,128)S(1)}, u32[]{:S(2)}, u32[]{:S(2)}) collective-permute-start(f32[8,1024]{1,0:T(8,128)S(1)} %add.175), channel_id=1, source_target_pairs={{0,4},{4,0},{8,12},{12,8},{16,20},{20,16},{24,28},{28,24},{1,5},{5... | collective-permute-start | bytes 98312 | tf_op jit(solution)/shard_map/ppermute | solution.py:303
  (42 other events, 308.3 us)
where the time goes:
time: 281 us; the launch traced here: 280 us
  Pallas kernels  156 us (56%)
  starting transfers between devices  51.1 us (18%)
  waiting for transfers between devices  23.8 us (8%)
  other arithmetic  18.4 us (7%)
  matrix products  16 us (6%)
  local copies, waits for them, and re-layouts  8.72 us (3%)
  between operations  5.43 us (2%)
    ppermute x50, starting transfers between devices, swap(): return lax.ppermute(value, axis, [(i, i ^ offset) for i in range(size)])  51.1 us
    pallas_call x6, Pallas kernels, place_rows(): call(functools.partial(place_body, tuple(starts)), (step,), in_specs, pl....  44.8 us
    ppermute x50, waiting for transfers between devices, swap(): return lax.ppermute(value, axis, [(i, i ^ offset) for i in range(size)])  23.8 us
    pallas_call x2, Pallas kernels, paired(): call(functools.partial(middle_pair_body, stream), (2,), specs + [whole(w_...  23 us
    pallas_call x2, Pallas kernels, paired(): call(functools.partial(front_pair_body, heads, length // 4, 4 * stream),...  21.2 us
    dot_general x4, matrix products, dot(): lax.dot_general(left, right, (on, ((), ())), preferred_element_type=F32)  16 us
    pallas_call x2, Pallas kernels, paired(): call(functools.partial(back_pair_body, heads, stream), (2,), [pl.BlockSpe...  15.8 us
    convert_element_type x13, other arithmetic, add(): return (left.astype(F32) + right.astype(F32)).astype(BF16)  13.1 us
  transfers between devices with their start and end apart: 50, of which 9 were waited for; matrix products, arithmetic and copies ran while one was open for 12% of the time, Pallas kernels for 56%

commit v1 on v0

--- a/solution.py
+++ b/solution.py
@@ -36,7 +36,7 @@
     "front": 5.2, "cot": 3.2, "middle": 5.5, "rows": 2.8, "outs": 3.9, "back": 1.0,
     "delta": 0.01, "mlp": 0.01, "last": 0.33, "put_own": 0.01, "put_out": 2.4, "put_grad": 2.4, "join": 1.5,
 }
-RATE = 1.5e9
+RATE = 4e9
 
 
 def call(body, grid, in_specs, out_specs, out_shape, flops, nbytes, name, scratch=(), alias=None):

time: 281 us -> 278 us (0.989)
    unnamed x80 -> x70, local copies, waits for them, and re-layouts: 7.59 us -> 7.64 us
where the time goes in v1:
time: 278 us; the launch traced here: 277 us
  Pallas kernels  156 us (56%)
  starting transfers between devices  51.7 us (19%)
  waiting for transfers between devices  22.6 us (8%)
  other arithmetic  16.4 us (6%)
  matrix products  16.4 us (6%)
  local copies, waits for them, and re-layouts  8.76 us (3%)
  between operations  5.44 us (2%)
    ppermute x50, starting transfers between devices, swap(): return lax.ppermute(value, axis, [(i, i ^ offset) for i in range(size)])  51.7 us
    pallas_call x6, Pallas kernels, place_rows(): call(functools.partial(place_body, tuple(starts)), (step,), in_specs, pl....  44.8 us
    pallas_call x2, Pallas kernels, paired(): call(functools.partial(middle_pair_body, stream), (2,), specs + [whole(w_...  23 us
    ppermute x50, waiting for transfers between devices, swap(): return lax.ppermute(value, axis, [(i, i ^ offset) for i in range(size)])  22.6 us
    pallas_call x2, Pallas kernels, paired(): call(functools.partial(front_pair_body, heads, length // 4, 4 * stream),...  21.2 us
    dot_general x4, matrix products, dot(): lax.dot_general(left, right, (on, ((), ())), preferred_element_type=F32)  16.4 us
    pallas_call x2, Pallas kernels, paired(): call(functools.partial(back_pair_body, heads, stream), (2,), [pl.BlockSpe...  15.7 us
    pallas_call x1, Pallas kernels, paired(): call(cot_pair_body, (4,), [pl.BlockSpec((length, width), lambda i, w: (w[...  12.9 us
  transfers between devices with their start and end apart: 50, of which 9 were waited for; matrix products, arithmetic and copies ran while one was open for 12% of the time, Pallas kernels for 56%

profile of v1, /device:TPU:0, one launch (start us, length us, event | category | flops | bytes accessed | tf_op | source)
XLA Modules:
  0.0 277.1 jit_solution(4375844087968283289)
XLA Ops:
  0.6 3.0 %collective-permute-start.1 = (bf16[256,1024]{1,0:T(8,128)(2,1)}, bf16[256,1024]{1,0:T(8,128)(2,1)S(1)}, u32[]{:S(2)}, u32[]{:S(2)}) collective-permute-start(bf16[256,1024]{1,0:T(8,128)(2,1)} %refs_12_.5), channel_id=1, source_target_pairs={{0,1},{1,0},{2,3},{3,2},{4,5},{5,4},{6,7},{7,6},{8,9},{9,8},{10,11... | collective-permute-start | bytes 1572872 | tf_op jit(solution)/shard_map/ppermute | solution.py:303
  6.4 10.6 %front.2 = (bf16[2,2,2,128,1024]{4,3,2,1,0:T(8,128)(2,1)}, bf16[2,2,2,128,512]{4,3,2,1,0:T(8,128)(2,1)}, bf16[2,2,2,128,512]{4,3,2,1,0:T(8,128)(2,1)}, bf16[512,...) custom-call(s32[25]{0:T(128)} %compare_select_fusion.4.where, ...), custom_call_target="tpu_custom_call" | custom-call | flops 41600000000 | bytes 1 | tf_op jit(solution)/shard_map/front/pallas_call | solution.py:1184
  17.0 2.0 collective-permute-start
  20.5 10.6 %front.3 = (bf16[2,2,2,128,1024]{4,3,2,1,0:T(8,128)(2,1)}, bf16[2,2,2,128,512]{4,3,2,1,0:T(8,128)(2,1)}, bf16[2,2,2,128,512]{4,3,2,1,0:T(8,128)(2,1)}, bf16[512,...) custom-call(s32[25]{0:T(128)} %compare_select_fusion.4.where, ...), custom_call_target="tpu_custom_call", output_to_operand_aliasing={{0}: (8, {}), {1}: (9, {}), {2}: (10, {})} | custom-call | flops 41600000000 | bytes 1 | tf_op jit(solution)/shard_map/front/pallas_call | solution.py:1184
  32.7 1.8 collective-permute-start.5
  34.7 12.9 %cot.1 = (bf16[1024,1024]{1,0:T(8,128)(2,1)}, bf16[1024,1024]{1,0:T(8,128)(2,1)}, f32[1024,1024]{1,0:T(8,128)}) custom-call(s32[25]{0:T(128)} %compare_select_fusion.4.where, bf16[8192,1024]{1,0:T(8,128)(2,1)} %source.11, bf16[8192,1024]{1,0:T(8,128)(2,1)} %source.11, s32[8,128]{1,0:T(8,128)} %routes.11, bf16[1024,1024]{1,0:T(8,128)(2,1)} %bitcast.43, ...), custom_call_target="tpu_custom_call" | custom-call | flops 51200000000 | bytes 1 | tf_op jit(solution)/shard_map/cot/pallas_call | solution.py:1230
  47.7 1.8 collective-permute-start.6
  50.6 11.4 %middle.2 = (f32[128,1024]{1,0:T(8,128)}, bf16[2,2,2,128,1024]{4,3,2,1,0:T(8,128)(2,1)}, bf16[2,2,2,128,1024]{4,3,2,1,0:T(8,128)(2,1)}, bf16[2,2,2,128,1024]{4,3...) custom-call(s32[25]{0:T(128)} %compare_select_fusion.4.where, ...), custom_call_target="tpu_custom_call" | custom-call | flops 44000002048 | bytes 1 | tf_op jit(solution)/shard_map/middle/pallas_call | solution.py:1280
  62.0 1.8 collective-permute-start.10
  64.6 11.7 %middle.3 = (f32[128,1024]{1,0:T(8,128)}, bf16[2,2,2,128,1024]{4,3,2,1,0:T(8,128)(2,1)}, bf16[2,2,2,128,1024]{4,3,2,1,0:T(8,128)(2,1)}, bf16[2,2,2,128,1024]{4,3...) custom-call(s32[25]{0:T(128)} %compare_select_fusion.4.where, ...), custom_call_target="tpu_custom_call", output_to_operand_aliasing={{1}: (14, {}), {2}: (15, {}), {3}: (16, {}), {4}: (17, {}),... | custom-call | flops 44000002048 | bytes 1 | tf_op jit(solution)/shard_map/middle/pallas_call | solution.py:1280
  76.3 1.6 collective-permute-start.9
  77.9 6.1 %convolution_convert_fusion.1 = bf16[1024,1024]{1,0:T(8,128)(2,1)} fusion(bf16[1024,1024]{1,0:T(8,128)(2,1)} %bitcast.55, bf16[1024,1024]{1,0:T(8,128)(2,1)} %bitcast.57), kind=kOutput, calls=%fused_computation.5 | convolution fusion | flops 2148532224 | bytes 6291456 | tf_op jit(solution)/shard_map/dot_general | solution.py:20
  84.0 7.3 %mlp.1 = (bf16[256,1024]{1,0:T(8,128)(2,1)}, bf16[256,1024]{1,0:T(8,128)(2,1)}, bf16[256,1024]{1,0:T(8,128)(2,1)}, bf16[256,1024]{1,0:T(8,128)(2,1)}) custom-call(s32[25]{0:T(128)} %compare_select_fusion.4.where, bf16[1024,1024]{1,0:T(8,128)(2,1)} %bitcast.47, bf16[1024,1024]{1,0:T(8,128)(2,1)} %w_down.1), custom_call_target="tpu_custom_call" | custom-call | flops 160000000 | bytes 1 | tf_op jit(solution)/shard_map/mlp/pallas_call | solution.py:1317
  93.7 1.7 collective-permute-start.13
  95.4 4.6 %convolution_convert_fusion = bf16[1024,1024]{1,0:T(8,128)(2,1)S(1)} fusion(bf16[1024,1024]{1,0:T(8,128)(2,1)} %bitcast.56, bf16[1024,1024]{1,0:T(8,128)(2,1)} %bitcast.58), kind=kOutput, calls=%fused_computation.4 | convolution fusion | flops 2148532224 | bytes 6291456 | tf_op jit(solution)/shard_map/dot_general | solution.py:20
  101.8 1.6 collective-permute-start.12
  104.8 6.5 %rows.1 = (f32[256,1024]{1,0:T(8,128)}, bf16[256,1024]{1,0:T(8,128)(2,1)}, f32[8,1024]{1,0:T(8,128)}, bf16[256,256]{1,0:T(8,128)(2,1)}, bf16[256,256]{1,0:T(8,12...) custom-call(s32[25]{0:T(128)} %compare_select_fusion.4.where, ...), custom_call_target="tpu_custom_call" | custom-call | flops 22400000000 | bytes 1 | tf_op jit(solution)/shard_map/rows/pallas_call | solution.py:1341
  114.9 3.8 %outs.1 = (bf16[4,128,1024]{2,1,0:T(8,128)(2,1)}, bf16[4,128,1024]{2,1,0:T(8,128)(2,1)}) custom-call(s32[25]{0:T(128)} %compare_select_fusion.4.where, bf16[512,256]{1,0:T(8,128)(2,1)} %get-tuple-element.142.refs_0_, bf16[512,256]{1,0:T(8,128)(2,1)} %copy-done.20, bf16[512,256]{1,0:T(8,128)(2,1)} %copy-done.21, bf16[512,256]{1,0:T(8,128)(2,1)} %copy-done.23, ...), custom_call_target="tpu_custom_call" | custom-call | flops 15600000000 | bytes 1 | tf_op jit(solution)/shard_map/outs/pallas_call | solution.py:1363
  121.1 1.9 collective-permute-start.25
  123.0 3.7 %collective-permute-done.12 = bf16[512,1024]{1,0:T(8,128)(2,1)} collective-permute-done((bf16[512,1024]{1,0:T(8,128)(2,1)S(1)}, bf16[512,1024]{1,0:T(8,128)(2,1)}, u32[]{:S(2)}, u32[]{:S(2)}) %collective-permute-start.12) | collective-permute-done | bytes 1048608 | tf_op jit(solution)/shard_map/ppermute | solution.py:303
  126.7 2.2 add_convert_fusion.1
  128.9 2.6 collective-permute-start.28
  131.5 7.7 %back.2 = (bf16[2,2,2,128,768]{4,3,2,1,0:T(8,128)(2,1)}, bf16[2,128,1024]{2,1,0:T(8,128)(2,1)}, bf16[2,128,1024]{2,1,0:T(8,128)(2,1)}) custom-call(s32[25]{0:T(128)} %compare_select_fusion.4.where, bf16[512,768]{1,0:T(8,128)(2,1)} %get-tuple-element.199.qkv, bf16[512,128]{1,0:T(8,128)(2,1)} %get-tuple-element.200.mask, f32[512,128]{1,0:T(8,128)} %get-tuple-element.201.lse, ...), custom_call_target="tpu_custom_call" | custom-call | flops 8000000000 | bytes 1 | tf_op jit(solution)/shard_map/back/pallas_call | solution.py:1385
  139.8 8.0 %back.3 = (bf16[2,2,2,128,768]{4,3,2,1,0:T(8,128)(2,1)}, bf16[2,128,1024]{2,1,0:T(8,128)(2,1)}, bf16[2,128,1024]{2,1,0:T(8,128)(2,1)}) custom-call(s32[25]{0:T(128)} %compare_select_fusion.4.where, bf16[512,768]{1,0:T(8,128)(2,1)} %get-tuple-element.207.qkv, bf16[512,128]{1,0:T(8,128)(2,1)} %get-tuple-element.208.mask, ...), custom_call_target="tpu_custom_call", output_to_operand_aliasing={{0}: (9, {})} | custom-call | flops 8000000000 | bytes 1 | tf_op jit(solution)/shard_map/back/pallas_call | solution.py:1385
  147.8 3.8 %bitcast_convert_fusion.1 = bf16[512,768]{1,0:T(8,128)(2,1)} fusion(bf16[2,2,2,128,512]{4,3,2,1,0:T(8,128)(2,1)} %get-tuple-element.205, bf16[2,2,2,128,768]{4,3,2,1,0:T(8,128)(2,1)} %get-tuple-element.211), kind=kOutput, calls=%fused_computation.7 | convolution fusion | flops 805699584 | bytes 3407872 | tf_op jit(solution)/shard_map/dot_general | solution.py:20
  153.5 1.9 bitcast_convert_fusion
  155.4 2.0 add_convert_fusion.4
  159.4 4.6 %delta.1 = (bf16[256,1024]{1,0:T(8,128)(2,1)}, f32[256,1024]{1,0:T(8,128)}, f32[8,1024]{1,0:T(8,128)}) custom-call(s32[25]{0:T(128)} %compare_select_fusion.4.where, bf16[256,1024]{1,0:T(8,128)(2,1)} %get-tuple-element.175.refs_0_, bf16[256,1024]{1,0:T(8,128)(2,1)} %collective-permute-done.13.refs_1_, bf16[256,1024]{1,0:T(8,128)(2,1)} %collective-permute-done.24.refs_2_, ...), custom_call_target="tpu_custom_call" | custom-call | flops 80000000 | bytes 1 | tf_op jit(solution)/shard_map/delta/pallas_call | solution.py:1432
  164.0 3.0 %collective-permute-done.23.refs_4_ = bf16[2,128,1024]{2,1,0:T(8,128)(2,1)} collective-permute-done((bf16[2,128,1024]{2,1,0:T(8,128)(2,1)}, bf16[2,128,1024]{2,1,0:T(8,128)(2,1)}, u32[]{:S(2)}, u32[]{:S(2)}) %collective-permute-start.23) | collective-permute-done | bytes 524320 | tf_op jit(solution)/shard_map/ppermute | solution.py:303
  166.9 1.8 fusion.4
  170.1 2.5 collective-permute-done.22
  172.6 1.9 fusion.5
  175.1 1.9 add_convert_fusion.7
  176.9 1.6 collective-permute-start.26
  178.5 6.1 %put_own.2.refs_2_ = bf16[8192,1024]{1,0:T(8,128)(2,1)} custom-call(s32[25]{0:T(128)} %compare_select_fusion.4.where, bf16[8192,1024]{1,0:T(8,128)(2,1)} %source.10, s32[8,128]{1,0:T(8,128)} %routes.11, bf16[256,1024]{1,0:T(8,128)(2,1)} %get-tuple-element.243.refs_0_), custom_call_target="tpu_custom_call" | custom-call | flops 80000000 | bytes 1 | tf_op jit(solution)/shard_map/put_own/pallas_call | solution.py:1009
  189.6 4.2 %last.1.refs_0_ = bf16[272,1024]{1,0:T(8,128)(2,1)} custom-call(s32[25]{0:T(128)} %compare_select_fusion.4.where, bf16[2,128,1024]{2,1,0:T(8,128)(2,1)} %get-tuple-element.203.refs_0_, bf16[2,128,1024]{2,1,0:T(8,128)(2,1)} %copy-done.9, bf16[128,1024]{1,0:T(8,128)(2,1)} %collective-permute-done.29.refs_2_, bf16[2,128,1024]{2,1,0:T(8,128)(2,1)} %get-tuple-element.215.refs_3_, ...), custom_call_target="tpu_custom_call" | custom-call | flops 3960000000 | bytes 1 | tf_op jit(solution)/shard_map/last/pallas_call | solution.py:1467
  193.9 6.6 %put_own.3.refs_2_ = bf16[8192,1024]{1,0:T(8,128)(2,1)} custom-call(s32[25]{0:T(128)} %compare_select_fusion.4.where, bf16[8192,1024]{1,0:T(8,128)(2,1)} %source.11, s32[8,128]{1,0:T(8,128)} %routes.11, bf16[272,1024]{1,0:T(8,128)(2,1)} %last.1.refs_0_), custom_call_target="tpu_custom_call" | custom-call | flops 80000000 | bytes 1 | tf_op jit(solution)/shard_map/put_own/pallas_call | solution.py:1009
  204.8 10.1 %put_out.2.refs_1_ = bf16[8192,1024]{1,0:T(8,128)(2,1)} custom-call(s32[25]{0:T(128)} %compare_select_fusion.4.where, bf16[8192,1024]{1,0:T(8,128)(2,1)} %source.10, s32[8,128]{1,0:T(8,128)} %routes.11, bf16[256,1024]{1,0:T(8,128)(2,1)} %collective-permute-done.31.refs_0_, ...), custom_call_target="tpu_custom_call", output_to_operand_aliasing={{}: (5, {})} | custom-call | flops 38400000000 | bytes 1 | tf_op jit(solution)/shard_map/put_out/pallas_call | solution.py:1009
  214.9 3.5 %collective-permute-done.34.refs_1_ = bf16[272,1024]{1,0:T(8,128)(2,1)} collective-permute-done((bf16[272,1024]{1,0:T(8,128)(2,1)S(1)}, bf16[272,1024]{1,0:T(8,128)(2,1)}, u32[]{:S(2)}, u32[]{:S(2)}) %collective-permute-start.34) | collective-permute-done | bytes 557088 | tf_op jit(solution)/shard_map/ppermute | solution.py:303
  219.8 10.0 %put_grad.2.refs_1_ = bf16[8192,1024]{1,0:T(8,128)(2,1)} custom-call(s32[25]{0:T(128)} %compare_select_fusion.4.where, bf16[8192,1024]{1,0:T(8,128)(2,1)} %source.11, s32[8,128]{1,0:T(8,128)} %routes.11, bf16[272,1024]{1,0:T(8,128)(2,1)} %collective-permute-done.33.refs_0_, ...), custom_call_target="tpu_custom_call", output_to_operand_aliasing={{}: (5, {})} | custom-call | flops 38400000000 | bytes 1 | tf_op jit(solution)/shard_map/put_grad/pallas_call | solution.py:1009
  229.8 1.6 collective-permute-start.38
  231.4 6.1 %put_out.3 = bf16[8192,1024]{1,0:T(8,128)(2,1)} custom-call(s32[25]{0:T(128)} %compare_select_fusion.4.where, bf16[8192,1024]{1,0:T(8,128)(2,1)} %source.10, s32[8,128]{1,0:T(8,128)} %routes.11, bf16[256,1024]{1,0:T(8,128)(2,1)} %collective-permute-done.35.refs_0_, bf16[8192,1024]{1,0:T(8,128)(2,1)} %put_out.2.refs_1_), custom_call_target="tpu_custom_call", output_to_operand_aliasing={{}: (4, {})} | custom-call | flops 19200000000 | bytes 1 | tf_op jit(solution)/shard_map/put_out/pallas_call | solution.py:1009
  239.1 6.1 %put_grad.3 = bf16[8192,1024]{1,0:T(8,128)(2,1)} custom-call(s32[25]{0:T(128)} %compare_select_fusion.4.where, bf16[8192,1024]{1,0:T(8,128)(2,1)} %source.11, s32[8,128]{1,0:T(8,128)} %routes.11, bf16[272,1024]{1,0:T(8,128)(2,1)} %collective-permute-done.36.refs_0_, bf16[8192,1024]{1,0:T(8,128)(2,1)} %put_grad.2.refs_1_), custom_call_target="tpu_custom_call", output_to_operand_aliasing={{}: (4, {})} | custom-call | flops 19200000000 | bytes 1 | tf_op jit(solution)/shard_map/put_grad/pallas_call | solution.py:1009
  245.4 1.6 collective-permute-start.44
  247.0 2.6 collective-permute-start.47
  250.9 7.0 %join.2 = (f32[1024,1024]{1,0:T(8,128)}, f32[1024,1024]{1,0:T(8,128)}) custom-call(s32[25]{0:T(128)} %compare_select_fusion.4.where, bf16[512,1024]{1,0:T(8,128)(2,1)} %copy-done.1, bf16[512,1024]{1,0:T(8,128)(2,1)} %collective-permute-done.42.side, bf16[512,1024]{1,0:T(8,128)(2,1)} %collective-permute-done.41.pair, bf16[512,1024]{1,0:T(8,128)(2,1)} %copy-done.14), custom_call_target="tpu_custom_call" | custom-call | flops 24000000000 | bytes 1 | tf_op jit(solution)/shard_map/join/pallas_call | solution.py:1040
  258.0 5.3 %collective-permute-done.44.refs_2_ = bf16[256,768]{1,0:T(8,128)(2,1)} collective-permute-done((bf16[256,768]{1,0:T(8,128)(2,1)S(1)}, bf16[256,768]{1,0:T(8,128)(2,1)}, u32[]{:S(2)}, u32[]{:S(2)}) %collective-permute-start.44) | collective-permute-done | bytes 393248 | tf_op jit(solution)/shard_map/ppermute | solution.py:303
  267.0 4.7 %join.3 = (f32[1024,768]{1,0:T(8,128)}, f32[256,1024]{1,0:T(8,128)}) custom-call(s32[25]{0:T(128)} %compare_select_fusion.4.where, bf16[256,768]{1,0:T(8,128)(2,1)} %copy-done.6, bf16[256,768]{1,0:T(8,128)(2,1)} %copy-done.18, bf16[256,768]{1,0:T(8,128)(2,1)} %collective-permute-done.44.refs_2_, bf16[256,768]{1,0:T(8,128)(2,1)} %copy-done.19, ...), custom_call_target="tpu_custom_call" | custom-call | flops 24000000000 | bytes 1 | tf_op jit(solution)/shard_map/join/pallas_call | solution.py:1066
  (168 shorter events, 44.6 us)
Async XLA Ops:
  0.6 30.5 %collective-permute-start.1 = (bf16[256,1024]{1,0:T(8,128)(2,1)}, bf16[256,1024]{1,0:T(8,128)(2,1)S(1)}, u32[]{:S(2)}, u32[]{:S(2)}) collective-permute-start(bf16[256,1024]{1,0:T(8,128)(2,1)} %refs_12_.5), channel_id=1, source_target_pairs={{0,1},{1,0},{2,3},{3,2},{4,5},{5,4},{6,7},{7,6},{8,9},{9,8},{10,11... | collective-permute-start | bytes 1572872 | tf_op jit(solution)/shard_map/ppermute | solution.py:303
  3.7 27.5 %collective-permute-start.2 = (bf16[256,1024]{1,0:T(8,128)(2,1)}, bf16[256,1024]{1,0:T(8,128)(2,1)S(1)}, u32[]{:S(2)}, u32[]{:S(2)}) collective-permute-start(bf16[256,1024]{1,0:T(8,128)(2,1)} %refs_12_.5), channel_id=1, source_target_pairs={{0,2},{1,3},{2,0},{3,1},{4,6},{5,7},{6,4},{7,5},{8,10},{9,11},{10,... | collective-permute-start | bytes 1572872 | tf_op jit(solution)/shard_map/ppermute | solution.py:303
  5.2 26.0 %collective-permute-start.3 = (bf16[256,1024]{1,0:T(8,128)(2,1)}, bf16[256,1024]{1,0:T(8,128)(2,1)S(1)}, u32[]{:S(2)}, u32[]{:S(2)}) collective-permute-start(bf16[256,1024]{1,0:T(8,128)(2,1)} %refs_12_.5), channel_id=1, source_target_pairs={{0,3},{1,2},{2,1},{3,0},{4,7},{5,6},{6,5},{7,4},{8,11},{9,10},{10,... | collective-permute-start | bytes 1572872 | tf_op jit(solution)/shard_map/ppermute | solution.py:303
  17.0 15.7 %collective-permute-start = (bf16[512,256]{1,0:T(8,128)(2,1)}, bf16[512,256]{1,0:T(8,128)(2,1)S(1)}, u32[]{:S(2)}, u32[]{:S(2)}) collective-permute-start(bf16[512,256]{1,0:T(8,128)(2,1)} %get-tuple-element.142.refs_0_), channel_id=1, source_target_pairs={{0,1},{1,0},{2,3},{3,2},{4,5},{5,4},{6,7},{7,6},{8,9},{9,8},{10,11... | collective-permute-start | bytes 786440 | tf_op jit(solution)/shard_map/ppermute | solution.py:303
  19.0 30.8 %collective-permute-start.4 = (bf16[512,256]{1,0:T(8,128)(2,1)}, bf16[512,256]{1,0:T(8,128)(2,1)S(1)}, u32[]{:S(2)}, u32[]{:S(2)}) collective-permute-start(bf16[512,256]{1,0:T(8,128)(2,1)} %get-tuple-element.142.refs_0_), channel_id=1, source_target_pairs={{0,2},{1,3},{2,0},{3,1},{4,6},{5,7},{6,4},{7,5},{8,10},{9,11},{10,... | collective-permute-start | bytes 786440 | tf_op jit(solution)/shard_map/ppermute | solution.py:303
  32.7 17.1 %collective-permute-start.5 = (bf16[512,256]{1,0:T(8,128)(2,1)S(1)}, bf16[512,256]{1,0:T(8,128)(2,1)S(1)}, u32[]{:S(2)}, u32[]{:S(2)}) collective-permute-start(bf16[512,256]{1,0:T(8,128)(2,1)S(1)} %collective-permute-done.refs_1_), channel_id=1, source_target_pairs={{0,2},{1,3},{2,0},{3,1},{4,6},{5,7},{6,4},{7,5},{8,10},{9,11},{10,... | collective-permute-start | bytes 786440 | tf_op jit(solution)/shard_map/ppermute | solution.py:303
  34.5 15.0 %collective-permute-start.7 = (bf16[512,256]{1,0:T(8,128)(2,1)}, bf16[512,256]{1,0:T(8,128)(2,1)S(1)}, u32[]{:S(2)}, u32[]{:S(2)}) collective-permute-start(bf16[512,256]{1,0:T(8,128)(2,1)} %get-tuple-element.158.refs_0_.refs_4_), channel_id=1, source_target_pairs={{0,2},{1,3},{2,0},{3,1},{4,6},{5,7},{6,4},{7,5},{8,10},{9,11},{10,... | collective-permute-start | bytes 786440 | tf_op jit(solution)/shard_map/ppermute | solution.py:303
  47.7 16.1 %collective-permute-start.6 = (bf16[512,256]{1,0:T(8,128)(2,1)S(1)}, bf16[512,256]{1,0:T(8,128)(2,1)S(1)}, u32[]{:S(2)}, u32[]{:S(2)}) collective-permute-start(bf16[512,256]{1,0:T(8,128)(2,1)S(1)} %copy-done.22), channel_id=1, source_target_pairs={{0,1},{1,0},{2,3},{3,2},{4,5},{5,4},{6,7},{7,6},{8,9},{9,8},{10,11... | collective-permute-start | bytes 786440 | tf_op jit(solution)/shard_map/ppermute | solution.py:303
  49.5 14.3 %collective-permute-start.8 = (bf16[512,256]{1,0:T(8,128)(2,1)S(1)}, bf16[512,256]{1,0:T(8,128)(2,1)S(1)}, u32[]{:S(2)}, u32[]{:S(2)}) collective-permute-start(bf16[512,256]{1,0:T(8,128)(2,1)S(1)} %collective-permute-done.7.refs_2_.refs_6_), channel_id=1, source_target_pairs={{0,1},{1,0},{2,3},{3,2},{4,5},{5,4},{6,7},{7,6},{8,9},{9,8},{10,11... | collective-permute-start | bytes 786440 | tf_op jit(solution)/shard_map/ppermute | solution.py:303
  62.0 15.9 %collective-permute-start.10 = (bf16[2,128,1024]{2,1,0:T(8,128)(2,1)}, bf16[2,128,1024]{2,1,0:T(8,128)(2,1)S(1)}, u32[]{:S(2)}, u32[]{:S(2)}) collective-permute-start(bf16[2,128,1024]{2,1,0:T(8,128)(2,1)} %get-tuple-element.169), channel_id=1, source_target_pairs={{0,1},{1,0},{2,3},{3,2},{4,5},{5,4},{6,7},{7,6},{8,9},{9,8},{10,11... | collective-permute-start | bytes 1572872 | tf_op jit(solution)/shard_map/ppermute | solution.py:303
  76.3 15.0 %collective-permute-start.9 = (bf16[2,128,1024]{2,1,0:T(8,128)(2,1)}, bf16[2,128,1024]{2,1,0:T(8,128)(2,1)S(1)}, u32[]{:S(2)}, u32[]{:S(2)}) collective-permute-start(bf16[2,128,1024]{2,1,0:T(8,128)(2,1)} %get-tuple-element.167), channel_id=1, source_target_pairs={{0,2},{1,3},{2,0},{3,1},{4,6},{5,7},{6,4},{7,5},{8,10},{9,11},{10,... | collective-permute-start | bytes 1572872 | tf_op jit(solution)/shard_map/ppermute | solution.py:303
  92.9 7.2 %collective-permute-start.11 = (bf16[1024,1024]{1,0:T(8,128)(2,1)}, bf16[1024,1024]{1,0:T(8,128)(2,1)S(1)}, u32[]{:S(2)}, u32[]{:S(2)}) collective-permute-start(bf16[1024,1024]{1,0:T(8,128)(2,1)} %convolution_convert_fusion.1), channel_id=1, source_target_pairs={{0,4},{4,0},{8,12},{12,8},{16,20},{20,16},{24,28},{28,24},{1,5},{5... | collective-permute-start | bytes 6291464 | tf_op jit(solution)/shard_map/ppermute | solution.py:303
  92.9 10.5 %collective-permute-start.14 = (bf16[128,1024]{1,0:T(8,128)(2,1)S(1)}, bf16[128,1024]{1,0:T(8,128)(2,1)S(1)}, u32[]{:S(2)}, u32[]{:S(2)}) collective-permute-start(bf16[128,1024]{1,0:T(8,128)(2,1)S(1)} %fusion.1), channel_id=1, source_target_pairs={{0,2},{1,3},{2,0},{3,1},{4,6},{5,7},{6,4},{7,5},{8,10},{9,11},{10,... | collective-permute-start | bytes 786440 | tf_op jit(solution)/shard_map/ppermute | solution.py:303
  93.4 10.7 %collective-permute-start.15 = (bf16[128,1024]{1,0:T(8,128)(2,1)}, bf16[128,1024]{1,0:T(8,128)(2,1)S(1)}, u32[]{:S(2)}, u32[]{:S(2)}) collective-permute-start(bf16[128,1024]{1,0:T(8,128)(2,1)} %fusion.2), channel_id=1, source_target_pairs={{0,1},{1,0},{2,3},{3,2},{4,5},{5,4},{6,7},{7,6},{8,9},{9,8},{10,11... | collective-permute-start | bytes 786440 | tf_op jit(solution)/shard_map/ppermute | solution.py:303
  93.7 26.5 %collective-permute-start.13 = (bf16[256,1024]{1,0:T(8,128)(2,1)}, bf16[256,1024]{1,0:T(8,128)(2,1)}, u32[]{:S(2)}, u32[]{:S(2)}) collective-permute-start(bf16[256,1024]{1,0:T(8,128)(2,1)} %get-tuple-element.182), channel_id=1, source_target_pairs={{0,1},{1,0},{2,3},{3,2},{4,5},{5,4},{6,7},{7,6},{8,9},{9,8},{10,11... | collective-permute-start | bytes 1572872 | tf_op jit(solution)/shard_map/ppermute | solution.py:303
  101.8 24.9 %collective-permute-start.12 = (bf16[512,1024]{1,0:T(8,128)(2,1)S(1)}, bf16[512,1024]{1,0:T(8,128)(2,1)}, u32[]{:S(2)}, u32[]{:S(2)}) collective-permute-start(bf16[512,1024]{1,0:T(8,128)(2,1)S(1)} %add_convert_fusion.2), channel_id=1, source_target_pairs={{0,8},{4,12},{8,0},{12,4},{16,24},{20,28},{24,16},{28,20},{1,9},{5... | collective-permute-start | bytes 3145736 | tf_op jit(solution)/shard_map/ppermute | solution.py:303
  111.4 7.4 %collective-permute-start.16 = (bf16[256,256]{1,0:T(8,128)(2,1)}, bf16[256,256]{1,0:T(8,128)(2,1)S(1)}, u32[]{:S(2)}, u32[]{:S(2)}) collective-permute-start(bf16[256,256]{1,0:T(8,128)(2,1)} %get-tuple-element.187), channel_id=1, source_target_pairs={{0,1},{1,0},{2,3},{3,2},{4,5},{5,4},{6,7},{7,6},{8,9},{9,8},{10,11... | collective-permute-start | bytes 393224 | tf_op jit(solution)/shard_map/ppermute | solution.py:303
  111.9 6.9 %collective-permute-start.17 = (bf16[256,256]{1,0:T(8,128)(2,1)}, bf16[256,256]{1,0:T(8,128)(2,1)S(1)}, u32[]{:S(2)}, u32[]{:S(2)}) collective-permute-start(bf16[256,256]{1,0:T(8,128)(2,1)} %get-tuple-element.192), channel_id=1, source_target_pairs={{0,2},{1,3},{2,0},{3,1},{4,6},{5,7},{6,4},{7,5},{8,10},{9,11},{10,... | collective-permute-start | bytes 393224 | tf_op jit(solution)/shard_map/ppermute | solution.py:303
  113.5 6.7 %collective-permute-start.18 = (bf16[256,256]{1,0:T(8,128)(2,1)}, bf16[256,256]{1,0:T(8,128)(2,1)S(1)}, u32[]{:S(2)}, u32[]{:S(2)}) collective-permute-start(bf16[256,256]{1,0:T(8,128)(2,1)} %get-tuple-element.194), channel_id=1, source_target_pairs={{0,3},{1,2},{2,1},{3,0},{4,7},{5,6},{6,5},{7,4},{8,11},{9,10},{10,... | collective-permute-start | bytes 393224 | tf_op jit(solution)/shard_map/ppermute | solution.py:303
  118.8 32.8 %collective-permute-start.21 = (bf16[4,128,1024]{2,1,0:T(8,128)(2,1)}, bf16[4,128,1024]{2,1,0:T(8,128)(2,1)}, u32[]{:S(2)}, u32[]{:S(2)}) collective-permute-start(bf16[4,128,1024]{2,1,0:T(8,128)(2,1)} %get-tuple-element.214), channel_id=1, source_target_pairs={{0,4},{4,0},{8,12},{12,8},{16,20},{20,16},{24,28},{28,24},{1,5},{5... | collective-permute-start | bytes 3145736 | tf_op jit(solution)/shard_map/ppermute | solution.py:303
  120.2 37.2 %collective-permute-start.24 = (bf16[256,1024]{1,0:T(8,128)(2,1)}, bf16[256,1024]{1,0:T(8,128)(2,1)}, u32[]{:S(2)}, u32[]{:S(2)}) collective-permute-start(bf16[256,1024]{1,0:T(8,128)(2,1)} %get-tuple-element.221), channel_id=1, source_target_pairs={{0,2},{1,3},{2,0},{3,1},{4,6},{5,7},{6,4},{7,5},{8,10},{9,11},{10,... | collective-permute-start | bytes 1572872 | tf_op jit(solution)/shard_map/ppermute | solution.py:303
  121.1 37.7 %collective-permute-start.25 = (bf16[256,1024]{1,0:T(8,128)(2,1)}, bf16[256,1024]{1,0:T(8,128)(2,1)}, u32[]{:S(2)}, u32[]{:S(2)}) collective-permute-start(bf16[256,1024]{1,0:T(8,128)(2,1)} %get-tuple-element.224), channel_id=1, source_target_pairs={{0,3},{1,2},{2,1},{3,0},{4,7},{5,6},{6,5},{7,4},{8,11},{9,10},{10,... | collective-permute-start | bytes 1572872 | tf_op jit(solution)/shard_map/ppermute | solution.py:303
  128.9 55.7 %collective-permute-start.28 = (bf16[512,1024]{1,0:T(8,128)(2,1)S(1)}, bf16[512,1024]{1,0:T(8,128)(2,1)S(1)}, u32[]{:S(2)}, u32[]{:S(2)}) collective-permute-start(bf16[512,1024]{1,0:T(8,128)(2,1)S(1)} %add_convert_fusion.1), channel_id=1, source_target_pairs={{0,16},{4,20},{8,24},{12,28},{16,0},{20,4},{24,8},{28,12},{1,17},{... | collective-permute-start | bytes 3145736 | tf_op jit(solution)/shard_map/ppermute | solution.py:303
  139.2 12.6 %collective-permute-start.19 = (bf16[2,128,1024]{2,1,0:T(8,128)(2,1)}, bf16[2,128,1024]{2,1,0:T(8,128)(2,1)S(1)}, u32[]{:S(2)}, u32[]{:S(2)}) collective-permute-start(bf16[2,128,1024]{2,1,0:T(8,128)(2,1)} %get-tuple-element.204), channel_id=1, source_target_pairs={{0,1},{1,0},{2,3},{3,2},{4,5},{5,4},{6,7},{7,6},{8,9},{9,8},{10,11... | collective-permute-start | bytes 1572872 | tf_op jit(solution)/shard_map/ppermute | solution.py:303
  151.6 23.5 %collective-permute-start.20 = (bf16[512,768]{1,0:T(8,128)(2,1)}, bf16[512,768]{1,0:T(8,128)(2,1)}, u32[]{:S(2)}, u32[]{:S(2)}) collective-permute-start(bf16[512,768]{1,0:T(8,128)(2,1)} %bitcast_convert_fusion.1), channel_id=1, source_target_pairs={{0,4},{4,0},{8,12},{12,8},{16,20},{20,16},{24,28},{28,24},{1,5},{5... | collective-permute-start | bytes 2359304 | tf_op jit(solution)/shard_map/ppermute | solution.py:303
  151.8 15.1 %collective-permute-start.23 = (bf16[2,128,1024]{2,1,0:T(8,128)(2,1)}, bf16[2,128,1024]{2,1,0:T(8,128)(2,1)}, u32[]{:S(2)}, u32[]{:S(2)}) collective-permute-start(bf16[2,128,1024]{2,1,0:T(8,128)(2,1)} %get-tuple-element.218), channel_id=1, source_target_pairs={{0,2},{1,3},{2,0},{3,1},{4,6},{5,7},{6,4},{7,5},{8,10},{9,11},{10,... | collective-permute-start | bytes 1572872 | tf_op jit(solution)/shard_map/ppermute | solution.py:303
  157.4 15.1 %collective-permute-start.22 = (bf16[2,128,1024]{2,1,0:T(8,128)(2,1)}, bf16[2,128,1024]{2,1,0:T(8,128)(2,1)}, u32[]{:S(2)}, u32[]{:S(2)}) collective-permute-start(bf16[2,128,1024]{2,1,0:T(8,128)(2,1)} %add_convert_fusion.4), channel_id=1, source_target_pairs={{0,1},{1,0},{2,3},{3,2},{4,5},{5,4},{6,7},{7,6},{8,9},{9,8},{10,11... | collective-permute-start | bytes 1572872 | tf_op jit(solution)/shard_map/ppermute | solution.py:303
  158.8 30.3 %collective-permute-start.29 = (bf16[128,1024]{1,0:T(8,128)(2,1)S(1)}, bf16[128,1024]{1,0:T(8,128)(2,1)}, u32[]{:S(2)}, u32[]{:S(2)}) collective-permute-start(bf16[128,1024]{1,0:T(8,128)(2,1)S(1)} %fusion.3), channel_id=1, source_target_pairs={{0,2},{1,3},{2,0},{3,1},{4,6},{5,7},{6,4},{7,5},{8,10},{9,11},{10,... | collective-permute-start | bytes 786440 | tf_op jit(solution)/shard_map/ppermute | solution.py:303
  168.7 20.9 %collective-permute-start.30 = (bf16[128,1024]{1,0:T(8,128)(2,1)}, bf16[128,1024]{1,0:T(8,128)(2,1)}, u32[]{:S(2)}, u32[]{:S(2)}) collective-permute-start(bf16[128,1024]{1,0:T(8,128)(2,1)} %fusion.4), channel_id=1, source_target_pairs={{0,1},{1,0},{2,3},{3,2},{4,5},{5,4},{6,7},{7,6},{8,9},{9,8},{10,11... | collective-permute-start | bytes 786440 | tf_op jit(solution)/shard_map/ppermute | solution.py:303
  174.4 11.8 %collective-permute-start.27 = (bf16[128,1024]{1,0:T(8,128)(2,1)}, bf16[128,1024]{1,0:T(8,128)(2,1)}, u32[]{:S(2)}, u32[]{:S(2)}) collective-permute-start(bf16[128,1024]{1,0:T(8,128)(2,1)} %fusion.5), channel_id=1, source_target_pairs={{0,2},{1,3},{2,0},{3,1},{4,6},{5,7},{6,4},{7,5},{8,10},{9,11},{10,... | collective-permute-start | bytes 786440 | tf_op jit(solution)/shard_map/ppermute | solution.py:303
  176.9 23.5 %collective-permute-start.26 = (bf16[256,768]{1,0:T(8,128)(2,1)}, bf16[256,768]{1,0:T(8,128)(2,1)}, u32[]{:S(2)}, u32[]{:S(2)}) collective-permute-start(bf16[256,768]{1,0:T(8,128)(2,1)} %add_convert_fusion.7), channel_id=1, source_target_pairs={{0,8},{4,12},{8,0},{12,4},{16,24},{20,28},{24,16},{28,20},{1,9},{5... | collective-permute-start | bytes 1179656 | tf_op jit(solution)/shard_map/ppermute | solution.py:303
  184.5 17.6 %collective-permute-start.31 = (bf16[256,1024]{1,0:T(8,128)(2,1)}, bf16[256,1024]{1,0:T(8,128)(2,1)}, u32[]{:S(2)}, u32[]{:S(2)}) collective-permute-start(bf16[256,1024]{1,0:T(8,128)(2,1)} %get-tuple-element.243.refs_0_), channel_id=1, source_target_pairs={{0,1},{1,0},{2,3},{3,2},{4,5},{5,4},{6,7},{7,6},{8,9},{9,8},{10,11... | collective-permute-start | bytes 1572872 | tf_op jit(solution)/shard_map/ppermute | solution.py:303
  186.3 15.8 %collective-permute-start.32 = (bf16[256,1024]{1,0:T(8,128)(2,1)}, bf16[256,1024]{1,0:T(8,128)(2,1)}, u32[]{:S(2)}, u32[]{:S(2)}) collective-permute-start(bf16[256,1024]{1,0:T(8,128)(2,1)} %get-tuple-element.243.refs_0_), channel_id=1, source_target_pairs={{0,2},{1,3},{2,0},{3,1},{4,6},{5,7},{6,4},{7,5},{8,10},{9,11},{10,... | collective-permute-start | bytes 1572872 | tf_op jit(solution)/shard_map/ppermute | solution.py:303
  189.1 56.1 %collective-permute-start.42 = (bf16[512,1024]{1,0:T(8,128)(2,1)S(1)}, bf16[512,1024]{1,0:T(8,128)(2,1)}, u32[]{:S(2)}, u32[]{:S(2)}) collective-permute-start(bf16[512,1024]{1,0:T(8,128)(2,1)S(1)} %add_convert_fusion.value), channel_id=1, source_target_pairs={{0,8},{4,12},{8,0},{12,4},{16,24},{20,28},{24,16},{28,20},{1,9},{5... | collective-permute-start | bytes 3145736 | tf_op jit(solution)/shard_map/ppermute | solution.py:303
  201.7 35.8 %collective-permute-start.37 = (bf16[256,768]{1,0:T(8,128)(2,1)S(1)}, bf16[256,768]{1,0:T(8,128)(2,1)S(1)}, u32[]{:S(2)}, u32[]{:S(2)}) collective-permute-start(bf16[256,768]{1,0:T(8,128)(2,1)S(1)} %add_convert_fusion.6), channel_id=1, source_target_pairs={{0,16},{4,20},{8,24},{12,28},{16,0},{20,4},{24,8},{28,12},{1,17},{... | collective-permute-start | bytes 1179656 | tf_op jit(solution)/shard_map/ppermute | solution.py:303
  202.1 12.8 %collective-permute-start.33 = (bf16[272,1024]{1,0:T(8,128)(2,1)S(1)}, bf16[272,1024]{1,0:T(8,128)(2,1)}, u32[]{:S(2)}, u32[]{:S(2)}) collective-permute-start(bf16[272,1024]{1,0:T(8,128)(2,1)S(1)} %copy-done.5), channel_id=1, source_target_pairs={{0,1},{1,0},{2,3},{3,2},{4,5},{5,4},{6,7},{7,6},{8,9},{9,8},{10,11... | collective-permute-start | bytes 1671176 | tf_op jit(solution)/shard_map/ppermute | solution.py:303
  202.8 15.6 %collective-permute-start.34 = (bf16[272,1024]{1,0:T(8,128)(2,1)S(1)}, bf16[272,1024]{1,0:T(8,128)(2,1)}, u32[]{:S(2)}, u32[]{:S(2)}) collective-permute-start(bf16[272,1024]{1,0:T(8,128)(2,1)S(1)} %copy-done.5), channel_id=1, source_target_pairs={{0,2},{1,3},{2,0},{3,1},{4,6},{5,7},{6,4},{7,5},{8,10},{9,11},{10,... | collective-permute-start | bytes 1671176 | tf_op jit(solution)/shard_map/ppermute | solution.py:303
  203.5 26.3 %collective-permute-start.35 = (bf16[256,1024]{1,0:T(8,128)(2,1)}, bf16[256,1024]{1,0:T(8,128)(2,1)}, u32[]{:S(2)}, u32[]{:S(2)}) collective-permute-start(bf16[256,1024]{1,0:T(8,128)(2,1)} %collective-permute-done.31.refs_0_), channel_id=1, source_target_pairs={{0,2},{1,3},{2,0},{3,1},{4,6},{5,7},{6,4},{7,5},{8,10},{9,11},{10,... | collective-permute-start | bytes 1572872 | tf_op jit(solution)/shard_map/ppermute | solution.py:303
  218.4 19.3 %collective-permute-start.36 = (bf16[272,1024]{1,0:T(8,128)(2,1)}, bf16[272,1024]{1,0:T(8,128)(2,1)}, u32[]{:S(2)}, u32[]{:S(2)}) collective-permute-start(bf16[272,1024]{1,0:T(8,128)(2,1)} %collective-permute-done.34.refs_1_), channel_id=1, source_target_pairs={{0,1},{1,0},{2,3},{3,2},{4,5},{5,4},{6,7},{7,6},{8,9},{9,8},{10,11... | collective-permute-start | bytes 1671176 | tf_op jit(solution)/shard_map/ppermute | solution.py:303
  229.8 7.6 %collective-permute-start.38 = (bf16[128,1024]{1,0:T(8,128)(2,1)S(1)}, bf16[128,1024]{1,0:T(8,128)(2,1)S(1)}, u32[]{:S(2)}, u32[]{:S(2)}) collective-permute-start(bf16[128,1024]{1,0:T(8,128)(2,1)S(1)} %fusion), channel_id=1, source_target_pairs={{0,8},{4,12},{8,0},{12,4},{16,24},{20,28},{24,16},{28,20},{1,9},{5... | collective-permute-start | bytes 786440 | tf_op jit(solution)/shard_map/ppermute | solution.py:303
  237.7 12.3 %collective-permute-start.41 = (bf16[512,1024]{1,0:T(8,128)(2,1)S(1)}, bf16[512,1024]{1,0:T(8,128)(2,1)}, u32[]{:S(2)}, u32[]{:S(2)}) collective-permute-start(bf16[512,1024]{1,0:T(8,128)(2,1)S(1)} %add_convert_fusion.value), channel_id=1, source_target_pairs={{0,4},{4,0},{8,12},{12,8},{16,20},{20,16},{24,28},{28,24},{1,5},{5... | collective-permute-start | bytes 3145736 | tf_op jit(solution)/shard_map/ppermute | solution.py:303
  238.6 6.6 %collective-permute-start.39 = (f32[8,1024]{1,0:T(8,128)S(1)}, f32[8,1024]{1,0:T(8,128)S(1)}, u32[]{:S(2)}, u32[]{:S(2)}) collective-permute-start(f32[8,1024]{1,0:T(8,128)S(1)} %convert_add_fusion), channel_id=1, source_target_pairs={{0,8},{4,12},{8,0},{12,4},{16,24},{20,28},{24,16},{28,20},{1,9},{5... | collective-permute-start | bytes 98312 | tf_op jit(solution)/shard_map/ppermute | solution.py:303
  245.2 4.7 %collective-permute-start.45 = (bf16[512,1024]{1,0:T(8,128)(2,1)}, bf16[512,1024]{1,0:T(8,128)(2,1)S(1)}, u32[]{:S(2)}, u32[]{:S(2)}) collective-permute-start(bf16[512,1024]{1,0:T(8,128)(2,1)} %collective-permute-done.42.side), channel_id=1, source_target_pairs={{0,4},{4,0},{8,12},{12,8},{16,20},{20,16},{24,28},{28,24},{1,5},{5... | collective-permute-start | bytes 3145736 | tf_op jit(solution)/shard_map/ppermute | solution.py:303
  245.4 17.8 %collective-permute-start.44 = (bf16[256,768]{1,0:T(8,128)(2,1)S(1)}, bf16[256,768]{1,0:T(8,128)(2,1)}, u32[]{:S(2)}, u32[]{:S(2)}) collective-permute-start(bf16[256,768]{1,0:T(8,128)(2,1)S(1)} %add_convert_fusion.5.refs_0_), channel_id=1, source_target_pairs={{0,8},{4,12},{8,0},{12,4},{16,24},{20,28},{24,16},{28,20},{1,9},{5... | collective-permute-start | bytes 1179656 | tf_op jit(solution)/shard_map/ppermute | solution.py:303
  247.0 16.3 %collective-permute-start.47 = (bf16[128,1024]{1,0:T(8,128)(2,1)S(1)}, bf16[128,1024]{1,0:T(8,128)(2,1)S(1)}, u32[]{:S(2)}, u32[]{:S(2)}) collective-permute-start(bf16[128,1024]{1,0:T(8,128)(2,1)S(1)} %add_convert_fusion.10), channel_id=1, source_target_pairs={{0,16},{4,20},{8,24},{12,28},{16,0},{20,4},{24,8},{28,12},{1,17},{... | collective-permute-start | bytes 786440 | tf_op jit(solution)/shard_map/ppermute | solution.py:303
  249.6 13.6 %collective-permute-start.40 = (f32[8,1024]{1,0:T(8,128)S(1)}, f32[8,1024]{1,0:T(8,128)S(1)}, u32[]{:S(2)}, u32[]{:S(2)}) collective-permute-start(f32[8,1024]{1,0:T(8,128)S(1)} %add.174), channel_id=1, source_target_pairs={{0,16},{4,20},{8,24},{12,28},{16,0},{20,4},{24,8},{28,12},{1,17},{... | collective-permute-start | bytes 98312 | tf_op jit(solution)/shard_map/ppermute | solution.py:303
  250.0 13.3 %collective-permute-start.43 = (bf16[256,768]{1,0:T(8,128)(2,1)S(1)}, bf16[256,768]{1,0:T(8,128)(2,1)S(1)}, u32[]{:S(2)}, u32[]{:S(2)}) collective-permute-start(bf16[256,768]{1,0:T(8,128)(2,1)S(1)} %add_convert_fusion.5.refs_0_), channel_id=1, source_target_pairs={{0,4},{4,0},{8,12},{12,8},{16,20},{20,16},{24,28},{28,24},{1,5},{5... | collective-permute-start | bytes 1179656 | tf_op jit(solution)/shard_map/ppermute | solution.py:303
  263.9 7.8 %collective-permute-start.46 = (f32[8,1024]{1,0:T(8,128)S(1)}, f32[8,1024]{1,0:T(8,128)S(1)}, u32[]{:S(2)}, u32[]{:S(2)}) collective-permute-start(f32[8,1024]{1,0:T(8,128)S(1)} %add.175), channel_id=1, source_target_pairs={{0,4},{4,0},{8,12},{12,8},{16,20},{20,16},{24,28},{28,24},{1,5},{5... | collective-permute-start | bytes 98312 | tf_op jit(solution)/shard_map/ppermute | solution.py:303
  (37 other events, 274.1 us)
